TPU v7x, 32 devices: a whole 2x2x4 slice. The times are simulated.
32 devices in a mesh: groups: 2 (over y), shard: 16 (over z, x, core).
Axes of the slice: x: 2, y: 2, z: 4, core: 2. Of those that a mesh axis runs over, the one named last changes fastest.
Arguments:
- traces: float32 [20736, 2048], P(('groups', 'shard')), parts along dimension 0, may hold values from -250 to 250
- cable_depth: float32 [32], P(('groups', 'shard')), parts along dimension 0, may hold values from 6 to 25
- receiver: int32 [20736], P(('groups', 'shard')), parts along dimension 0, may hold values from 0 to 671, as said below
- shot_slot: int32 [32], P('groups'), parts along dimension 0, may hold values from 0 to 15, as said below
- gather_home: int32 [1344], P('groups'), parts along dimension 0, may hold values from 0 to 671, each once
Outputs:
- filtered_gathers: float32 [1344, 16, 2048], P(('groups', 'shard')), parts along dimension 0
There are 2 independent parts, one for each index of `groups`. A program takes and returns all parts, laid end to end along the dimension named above; each array names one. Nothing has to cross between parts.
Inputs may be any that keep to these rules, and one draw needn't show every extreme that they name: The 648 receiver bins of one record are distinct. `shot_slot`: every record has a position of its own.
All inputs are finite; a program needn't handle non-finite values.
Results may differ from a plain program's by a relative error of at most 0.0081.
Values may be sent and summed in bfloat16 or wider, within the bound.
No kernel may reach another device: no remote copies, remote signals or barrier semaphores. Data moves between devices by JAX's collectives and lax.ppermute only.
A program may use at most 64 MiB of HBM per device.

v0:
```python
import math

import jax
import jax.numpy as jnp
import ml_dtypes
import numpy as np
from jax import lax
from jax.experimental import pallas as pl
from jax.experimental.pallas import tpu as pltpu
from jax.sharding import PartitionSpec as P


FREQ = 576

sample_step = 0.002
water_speed = 1500.0
channel_spacing = 12.5
shot_spacing = 25.0
surface_reflect = 0.9
ghost_floor = 0.1
reject_speed = 1500.0
low_floor = 4.0 * math.pi
energy_eps = 1e-06

BF = jnp.bfloat16
F32 = jnp.float32
LANES = 128
HALF = 64
UNIT = 8
ALL_VMEM = 60 << 20
MOST_VMEM = 53 << 20
FRONT_VMEM = 52 << 20
PART_VMEM = 36 << 20


def to_bf16(table):
    return np.asarray(table, np.float32).astype(ml_dtypes.bfloat16)


def bin_tiles():
    even = np.arange(0, FREQ, 2)
    odd = np.arange(1, FREQ, 2)
    whole = len(even) // HALF
    left = len(even) - whole * HALF
    assert 2 * left == HALF and len(odd) == len(even)
    even_tiles = [even[j * HALF : (j + 1) * HALF] for j in range(whole)]
    odd_tiles = [odd[left + j * HALF : left + (j + 1) * HALF] for j in range(whole)]
    mixed = np.concatenate([even[whole * HALF :], odd[:left]])
    return even_tiles, odd_tiles, mixed


def time_table(n_samples, tiles, parity):
    samples = np.arange(n_samples // 2, dtype=np.int64)
    parts = []
    for bins in tiles:
        angle = (samples[:, None] * bins[None, :] % n_samples) * (2.0 * np.pi / n_samples)
        keep = (bins % 2 == parity).astype(np.float64)[None, :]
        parts += [np.cos(angle) * keep, -np.sin(angle) * keep]
    return to_bf16(np.concatenate(parts, axis=1))


def wave_rows(n_channels):
    return -(-(n_channels // 2 + 1) // 16) * 16


def wave_table(n_channels):
    rows = wave_rows(n_channels)
    k = np.arange(rows, dtype=np.int64)
    c = np.arange(n_channels, dtype=np.int64)
    angle = (k[:, None] * c[None, :] % n_channels) * (2.0 * np.pi / n_channels)
    live = (k <= n_channels // 2)[:, None]
    inner = ((k > 0) & (2 * k < n_channels))[:, None]
    return to_bf16(np.concatenate([np.cos(angle) * live, np.sin(angle) * inner], axis=0))


def vertical_table(n_channels, n_samples, tiles):
    rows = wave_rows(n_channels)
    k = np.minimum(np.arange(rows), n_channels // 2).astype(np.float64)
    kx = 2.0 * np.pi * k / (n_channels * channel_spacing)
    bins = np.concatenate(tiles).astype(np.float64)
    slow = 2.0 * np.pi * bins / (n_samples * sample_step) / water_speed
    return (2.0 * np.sqrt(np.maximum(slow[None, :] ** 2 - kx[:, None] ** 2, 0.0))).astype(np.float32)


def shot_basis(records):
    k = np.concatenate([np.arange(records + 1), np.arange(1, records)])
    p = np.arange(records)
    angle = (k[:, None] * p[None, :] % (2 * records)) * (np.pi / records)
    is_sin = (np.arange(2 * records) > records)[:, None]
    return np.where(is_sin, np.sin(angle), np.cos(angle)), k


def shot_forward(records, block):
    basis, _ = shot_basis(records)
    full = np.einsum("kp,gh->gkph", basis, np.eye(block))
    return to_bf16(full.reshape(block * 2 * records, records * block))


def shot_inverse(records):
    basis, _ = shot_basis(records)
    full = np.einsum("kp,gh->gphk", basis, np.eye(UNIT))
    return to_bf16(full.reshape(UNIT * records, UNIT * 2 * records))


def response_table(records, n_samples, tiles):
    _, k = shot_basis(records)
    single = (k == 0) | (k == records)
    parts = []
    for bins in tiles:
        angular = 2.0 * np.pi * bins.astype(np.float64) / (n_samples * sample_step)
        shot_number = 2.0 * np.pi * k / (2 * records * shot_spacing)
        ratio = reject_speed * shot_number[:, None] / (angular[None, :] + low_floor)
        value = 1.0 / (1.0 + ratio**4) / (2.0 * records)
        value = value * np.where(single, 1.0, 2.0)[:, None] * np.where(bins == 0, 1.0, 2.0)[None, :]
        parts += [value, value]
    return np.concatenate(parts, axis=1).astype(np.float32)


def sin_cos(angle):
    turns = jnp.floor(angle * (2.0 / math.pi) + 0.5)
    rest = ((angle - turns * 1.5703125) - turns * 4.837512969970703125e-4) - turns * 7.54978995489188216e-8
    sq = rest * rest
    sine = ((-1.9515295891e-4 * sq + 8.3321608736e-3) * sq - 1.6666654611e-1) * sq * rest + rest
    cosine = ((2.443315711809948e-5 * sq - 1.388731625493765e-3) * sq + 4.166664568298827e-2) * sq * sq - 0.5 * sq + 1.0
    quarter = turns.astype(jnp.int32)
    odd = (quarter & 1) == 1
    sin_out = jnp.where(odd, cosine, sine)
    cos_out = jnp.where(odd, sine, cosine)
    sin_out = jnp.where((quarter & 2) == 2, -sin_out, sin_out)
    cos_out = jnp.where(((quarter + 1) & 2) == 2, -cos_out, cos_out)
    return sin_out, cos_out


def gains(vertical, depth, weight):
    sine, cosine = sin_cos(vertical * depth)
    denominator = 1.0 - 2.0 * surface_reflect * cosine + surface_reflect * surface_reflect + ghost_floor
    scale = weight / denominator
    return (1.0 - surface_reflect * cosine) * scale, -surface_reflect * sine * scale


def tile_gains(gain_re, gain_im, second):
    lane = lax.broadcasted_iota(jnp.int32, gain_re.shape, 1)
    low = lane < HALF
    re_other = pltpu.roll(gain_re, HALF, 1)
    im_other = pltpu.roll(gain_im, HALF, 1)
    if second:
        return jnp.where(low, re_other, gain_re), jnp.where(low, -im_other, gain_im)
    return jnp.where(low, gain_re, re_other), jnp.where(low, -gain_im, im_other)


def dot(a, b):
    return jnp.dot(a, b, preferred_element_type=F32)


def lift(spec, factors_ref, first, wave_ref):
    rows = wave_ref.shape[0] // 2
    plain = dot(wave_ref[...], spec)
    lifted = []
    for t in range(spec.shape[1] // LANES):
        same = factors_ref[0, first + t]
        swapped = factors_ref[1, first + t]
        both = []
        for h in range(2):
            part = plain[h * rows : (h + 1) * rows, t * LANES : (t + 1) * LANES]
            both.append((part * same + pltpu.roll(part, HALF, 1) * swapped).astype(BF))
        lifted.append(jnp.concatenate(both, axis=0))
    return join(lifted)


def store_factors(factors_ref, vertical_ref, depth, n_channels):
    tiles = factors_ref.shape[1]
    row = lax.broadcasted_iota(jnp.int32, (vertical_ref.shape[0], LANES), 0)
    single = (row == 0) | (row * 2 == n_channels)
    weight = jnp.where(single, 1.0 / n_channels, 2.0 / n_channels)
    for t in range(0, tiles, 2):
        gain_re, gain_im = gains(vertical_ref[:, t * HALF : (t + 2) * HALF], depth, weight)
        for h in range(min(2, tiles - t)):
            factors_ref[0, t + h], factors_ref[1, t + h] = tile_gains(gain_re, gain_im, h == 1)


def join(parts):
    return parts[0] if len(parts) == 1 else jnp.concatenate(parts, axis=1)


def energy_of(cleaned):
    total = jnp.sum(cleaned * cleaned, axis=0, keepdims=True)
    return sum(total[:, t * LANES : (t + 1) * LANES] for t in range(cleaned.shape[1] // LANES))


class Layout:
    def __init__(self, per, tiles, spare):
        self.whole = per // UNIT
        self.left = per % UNIT
        self.tiles = tiles
        self.shared = UNIT // self.left if self.left else 1
        rows = tiles * self.left
        self.left_units = -(-tiles // self.shared) if self.left else 0
        if spare and rows - (self.left_units - 1) * self.shared * self.left == UNIT or spare and not self.left_units:
            self.left_units += 1
        self.units = self.whole * tiles + self.left_units

    def unit(self, tile, u):
        if u < self.whole:
            return tile * self.whole + u, 0
        if u == self.whole and self.left:
            return self.whole * self.tiles + tile // self.shared, tile % self.shared * self.left
        return None, 0


def partner(me, dz, lo, n, sign):
    return (me // 4 + (dz if sign > 0 else n - dz)) % n * 4 + ((me % 4) ^ lo)


def chips(records):
    n = records // 4
    far = sorted(range(1, n), key=lambda d: -min(d, n - d))
    return [2 * dz + dx for dz in far for dx in range(2)] + [1]


def place_message(placed, layout, frame, store, i, energy=None):
    mine = placed[i * frame : (i + 1) * frame]
    parts = [mine[: layout.whole * UNIT, t * LANES : (t + 1) * LANES] for t in range(layout.tiles)] if layout.whole else []
    left = [jnp.zeros((UNIT, LANES), F32) for _ in range(layout.left_units)]
    if layout.left:
        row = lax.broadcasted_iota(jnp.int32, (UNIT, LANES), 0)
        for t in range(layout.tiles):
            unit = mine[layout.whole * UNIT : (layout.whole + 1) * UNIT, t * LANES : (t + 1) * LANES]
            shift = t % layout.shared * layout.left
            unit = jnp.where(row < layout.left, unit, 0.0)
            left[t // layout.shared] += pltpu.roll(unit, shift, 0) if shift else unit
    if energy is not None:
        row = lax.broadcasted_iota(jnp.int32, (UNIT, LANES), 0)
        left[-1] = jnp.where(row == UNIT - 1, energy, left[-1])
    store(jnp.concatenate(parts + left, axis=0).astype(BF))


def split_energy(energy):
    total = jnp.sum(energy, axis=1, keepdims=True)
    high = total.astype(BF).astype(F32)
    middle = (total - high).astype(BF).astype(F32)
    low = total - high - middle
    lane = lax.broadcasted_iota(jnp.int32, (1, LANES), 1)
    return jnp.where(lane == 0, high, jnp.where(lane == 1, middle, jnp.where(lane == 2, low, 0.0)))


def into(ref, index=None):
    def store(value):
        if index is None:
            ref[...] = value
        else:
            ref[index] = value

    return store


def start_all(pairs, sems, first=0):
    copies = [pltpu.make_async_copy(a, b, sems.at[first + i]) for i, (a, b) in enumerate(pairs)]
    for c in copies:
        c.start()
    return copies


def front_kernel(per, frame, layout, records, count):
    def kernel(depth_ref, receiver_ref, home_ref, vertical_hbm, wave_hbm, traces_hbm, table_hbm, mixed_hbm, *refs):
        later_hbm = refs[:2]
        *messages, odd_ref, place_ref, wave_ref, energy_ref = refs[2 : 6 + count]
        later = refs[6 + count : 8 + count]
        vertical_ref, traces_ref, table_ref, mixed_ref, sum_ref, placed_ref, factors_ref, sems = refs[8 + count :]
        me = lax.axis_index("shard")
        n_channels, n_samples = traces_ref.shape
        half = n_samples // 2
        steps = 3
        step = n_channels // steps
        pairs = [(traces_hbm.at[pl.ds(s * step, step), :], traces_ref.at[pl.ds(s * step, step), :]) for s in range(steps)]
        pairs = [(vertical_hbm, vertical_ref), (wave_hbm, wave_ref), *pairs, (table_hbm, table_ref), (mixed_hbm, mixed_ref)]
        copies = start_all(pairs, sems)
        n_rec = home_ref.shape[0]
        home = home_ref[...].reshape(1, n_rec)
        device = jnp.floor((home.astype(F32) + 0.5) * (1.0 / per)).astype(jnp.int32)
        n = records // 4
        turn = (device >> 2) - me // 4
        turn = jnp.where(turn < 0, turn + n, turn)
        home_row = (turn * 4 + ((device & 3) ^ (me % 4))) * frame + (home - device * per)
        both = jnp.concatenate([home_row >> 7, home_row & 127, jnp.zeros((14, n_rec), jnp.int32)], axis=0).astype(F32).astype(BF)
        to_bin = lax.broadcasted_iota(jnp.int32, (n_rec, n_channels), 0) == receiver_ref[...].reshape(1, n_channels)
        target = dot(both, jnp.where(to_bin, 1.0, 0.0).astype(BF))
        target = (target[0:1] * 128.0 + target[1:2]).astype(jnp.int32)
        picked = lax.broadcasted_iota(jnp.int32, (records * frame, n_channels), 0) == target
        picked = jnp.where(picked, 1.0, 0.0).astype(BF)
        copies[0].wait()
        copies[1].wait()
        place_ref[...] = lax.dot_general(picked, wave_ref[...], (((1,), (1,)), ((), ())), preferred_element_type=F32).astype(BF)
        store_factors(factors_ref, vertical_ref, depth_ref[0], n_channels)
        outs = start_all(list(zip(later_hbm, later)), sems, len(copies))
        for s in range(steps):
            copies[2 + s].wait()
            part = pl.ds(s * step, step)
            first = traces_ref[part, :half]
            second = traces_ref[part, half:]
            sum_ref[part, :] = (first + second).astype(BF)
            odd_ref[part, :] = (first - second).astype(BF)
        copies[-2].wait()
        even = dot(sum_ref[...], table_ref[...])
        copies[-1].wait()
        whole = (layout.tiles - 1) * LANES
        mixed = even[:, whole:] + dot(odd_ref[...], mixed_ref[...])
        spec = jnp.concatenate([even[:, :whole].astype(BF), mixed.astype(BF)], axis=1)
        placed_ref[...] = dot(place_ref[...], lift(spec, factors_ref, 0, wave_ref))
        energy_ref[...] = energy_of(placed_ref[...])
        for i in range(records):
            store = into(messages[0], partner(me, i // 4, i % 4, n, 1)) if count == 1 else into(messages[i // 2], i % 2)
            place_message(placed_ref, layout, frame, store, i)
        for c in outs:
            c.wait()

    return kernel


def second_kernel(frame, layout, records):
    def kernel(depth_ref, energy_ref, odd_ref, place_ref, wave_ref, table_ref, vertical_ref, message_ref, placed_ref, factors_ref):
        me = lax.axis_index("shard")
        store_factors(factors_ref, vertical_ref, depth_ref[0], odd_ref.shape[0])
        spec = dot(odd_ref[...], table_ref[...]).astype(BF)
        placed_ref[...] = dot(place_ref[...], lift(spec, factors_ref, 0, wave_ref))
        pieces = split_energy(energy_ref[...] + energy_of(placed_ref[...]))
        for i in range(records):
            store = into(message_ref, partner(me, i // 4, i % 4, records // 4, 1))
            place_message(placed_ref, layout, frame, store, i, pieces)

    return kernel


def source_order(slot_ref, records, block, source):
    size = records * block
    column = lax.broadcasted_iota(jnp.int32, (1, size), 1)
    goal = jnp.zeros((1, size), jnp.int32)
    for i in range(records):
        goal = jnp.where(column // block == i, slot_ref[source(i)], goal)
    goal = goal * block + column % block
    return jnp.where(lax.broadcasted_iota(jnp.int32, (size, size), 0) == goal, 1.0, 0.0).astype(BF)


def filter_gathers(arrived, layout, forward_ref, inverse_ref, response_ref, out_ref, per, block):
    k = response_ref.shape[0]
    records = k // 2
    blank = jnp.zeros((UNIT, LANES), F32)
    units = [a.astype(F32) for a in arrived]
    for b in range(-(-per // block)):
        live = min(block, per - b * block)
        sides = []
        for t in range(layout.tiles):
            pieces = []
            for a in units:
                for u in range(b * block // UNIT, (b + 1) * block // UNIT):
                    at, up = layout.unit(t, u)
                    piece = blank if at is None else a[at * UNIT : (at + 1) * UNIT]
                    pieces.append(pltpu.roll(piece, UNIT - up, 0) if up else piece)
            sides.append(jnp.concatenate(pieces, axis=0).astype(BF))
        part = dot(forward_ref[: live * k, :], join(sides)).reshape(live, k, layout.tiles * LANES)
        part = part * response_ref[...][None]
        part = part.reshape(live * k, layout.tiles * LANES).astype(BF)
        for g in range(0, live, UNIT):
            some = min(UNIT, live - g)
            back = dot(inverse_ref[: some * records, : some * k], part[g * k : (g + some) * k])
            row = (b * block + g) * records
            out_ref[row : row + some * records, : layout.tiles * LANES] = back.astype(BF)


def repack_kernel(n):
    def kernel(*refs):
        for chip in range(n):
            refs[n][chip] = refs[chip][1]

    return kernel


def even_kernel(per, block, layout, records, n_sources):
    def kernel(slot_ref, forward_hbm, inverse_hbm, response_hbm, table_hbm, *refs):
        sources = refs[:n_sources]
        (out_hbm, forward_b_hbm, mixed_hbm, out_ref, forward_b_ref, forward_ref, plain_ref, inverse_ref, response_ref, table_ref,
         filtered_ref, sems) = refs[n_sources:]
        me = lax.axis_index("shard")
        n = records // 4
        arrived = []
        for i in range(records):
            if n_sources == 1:
                arrived.append(sources[0][i])
            elif i % 2:
                arrived.append(sources[-1][i // 2])
            else:
                arrived.append(sources[i // 2][0])
        pairs = [(forward_hbm, plain_ref), (inverse_hbm, inverse_ref), (response_hbm, response_ref), (table_hbm, table_ref)]
        copies = start_all(pairs, sems)
        copies[0].wait()
        forward_b_ref[...] = dot(plain_ref[...], source_order(slot_ref, records, block, lambda i: i)).astype(BF)
        if n_sources == 1:
            forward_ref[...] = forward_b_ref[...]
        else:
            order = source_order(slot_ref, records, block, lambda i: partner(me, i // 4, i % 4, n, -1))
            forward_ref[...] = dot(plain_ref[...], order).astype(BF)
        for c in copies[1:]:
            c.wait()
        filter_gathers(arrived, layout, forward_ref, inverse_ref, response_ref, filtered_ref, per, block)
        mixed = filtered_ref.at[:, pl.ds((layout.tiles - 1) * LANES, LANES)]
        outs = start_all([(forward_b_ref, forward_b_hbm), (mixed, mixed_hbm)], sems, 4)
        out_ref[...] = dot(filtered_ref[...], table_ref[...])
        for c in outs + start_all([(out_ref, out_hbm)], sems, 6):
            c.wait()

    return kernel


def last_kernel(per, block, layout, n_traces, records):
    def kernel(arrived_hbm, forward_hbm, inverse_hbm, response_hbm, mixed_hbm, odd_table_hbm, even_hbm,
               out_hbm, arrived_ref, forward_ref, inverse_ref, response_ref, odd_table_ref, even_ref, filtered_ref, out_ref, sems):
        half = even_ref.shape[1]
        strip = 256
        cuts = [pl.ds(s, strip) for s in range(0, half, strip)]
        mixed = filtered_ref.at[:, pl.ds(layout.tiles * LANES, LANES)]
        first = [(arrived_hbm, arrived_ref), (forward_hbm, forward_ref), (inverse_hbm, inverse_ref), (response_hbm, response_ref)]
        fetch = start_all(first + [(odd_table_hbm, odd_table_ref), (mixed_hbm, mixed)], sems)
        fetch += start_all([(even_hbm.at[:, c], even_ref.at[:, c]) for c in cuts], sems, len(fetch))
        for c in fetch[:4]:
            c.wait()
        arrived = [arrived_ref[s] for s in range(records)]
        row = lax.broadcasted_iota(jnp.int32, (UNIT, LANES), 0)
        lane = lax.broadcasted_iota(jnp.int32, (UNIT, LANES), 1)
        ends = sum(a[(layout.units - 1) * UNIT :].astype(F32) for a in arrived)
        ends = jnp.where((row == UNIT - 1) & (lane < 3), ends, 0.0)
        energy = jnp.sum(ends, keepdims=True)
        scale = lax.rsqrt(2.0 * FREQ * (energy * (1.0 / (n_traces * FREQ)) + energy_eps))
        filter_gathers(arrived, layout, forward_ref, inverse_ref, response_ref, filtered_ref, per, block)
        for c in fetch[4:6]:
            c.wait()
        copies = []
        for s in range(0, half, strip):
            fetch[6 + s // strip].wait()
            odd = dot(filtered_ref[...], odd_table_ref[:, s : s + strip])
            even = even_ref[:, s : s + strip]
            out_ref[:, s : s + strip] = (even + odd) * scale
            out_ref[:, half + s : half + s + strip] = (even - odd) * scale
            pairs = []
            for here in (pl.ds(s, strip), pl.ds(half + s, strip)):
                pairs.append((out_ref.at[:, here], out_hbm.at[:, here]))
            copies += start_all(pairs, sems, len(fetch) + len(copies))
        for c in copies:
            c.wait()

    return kernel


def shards(traces, cable_depth, receiver, shot_slot, gather_home):
    records = lax.axis_size("shard")
    n_rec = gather_home.shape[0]
    per = n_rec // records
    n_channels, n_samples = traces.shape
    half = n_samples // 2
    block = 2 * UNIT if records <= 16 else UNIT
    frame = -(-per // UNIT) * UNIT
    even_tiles, odd_tiles, mixed = bin_tiles()
    n_whole = len(even_tiles)
    layout = Layout(per, n_whole + 1, False)
    layout_b = Layout(per, n_whole, True)
    wave = wave_table(n_channels)
    even_table = time_table(n_samples, even_tiles + [mixed], 0)
    odd_table = time_table(n_samples, odd_tiles + [mixed], 1)
    mixed_odd = np.ascontiguousarray(odd_table[:, n_whole * LANES :])
    odd_whole = np.ascontiguousarray(odd_table[:, : n_whole * LANES])
    pad_bins = np.zeros((HALF,), np.int64)
    vertical = vertical_table(n_channels, n_samples, even_tiles + [mixed, pad_bins])
    vertical_b = vertical_table(n_channels, n_samples, odd_tiles)
    pairwise = records <= 16

    smem = pl.BlockSpec(memory_space=pltpu.SMEM)
    vmem = pl.BlockSpec(memory_space=pltpu.VMEM)
    hbm = pl.BlockSpec(memory_space=pltpu.HBM)
    alone = pltpu.CompilerParams(vmem_limit_bytes=ALL_VMEM)
    most = pltpu.CompilerParams(vmem_limit_bytes=MOST_VMEM)
    shared = pltpu.CompilerParams(vmem_limit_bytes=PART_VMEM)

    def scratch(array):
        return pltpu.VMEM(array.shape, array.dtype)

    n = records // 4
    planes = records // 2 if pairwise else 1
    *sources, odd, place, wave_kept, energy, odd_kept, vertical_kept = pl.pallas_call(
        front_kernel(per, frame, layout, records, planes),
        out_shape=(
            *(jax.ShapeDtypeStruct((records // planes, layout.units * UNIT, LANES), BF) for _ in range(planes)),
            pltpu.VMEM((n_channels, half), BF),
            pltpu.VMEM((records * frame, wave.shape[0]), BF),
            scratch(wave),
            pltpu.VMEM((1, LANES), F32),
            scratch(odd_whole),
            scratch(vertical_b),
        ),
        in_specs=[smem, vmem, vmem] + [hbm] * 7,
        out_specs=(vmem,) * (6 + planes),
        scratch_shapes=[
            scratch(vertical),
            scratch(traces),
            scratch(even_table),
            scratch(mixed_odd),
            pltpu.VMEM((n_channels, half), BF),
            pltpu.VMEM((records * frame, (n_whole + 1) * LANES), F32),
            pltpu.VMEM((2, n_whole + 1, wave.shape[0] // 2, LANES), F32),
            pltpu.SemaphoreType.DMA((10,)),
        ],
        compiler_params=pltpu.CompilerParams(vmem_limit_bytes=FRONT_VMEM),
        name="front",
    )(cable_depth, receiver, gather_home, vertical, wave, traces, even_table, mixed_odd, odd_whole, vertical_b)
    if pairwise:
        for chip in chips(records):
            route = [(s, partner(s, chip // 2, chip % 2 * 2, n, 1)) for s in range(records)]
            sources[chip] = lax.ppermute(sources[chip], "shard", route)
    else:
        sources = [lax.all_to_all(sources[0], "shard", split_axis=0, concat_axis=0, tiled=True)]

    second = pl.pallas_call(
        second_kernel(frame, layout_b, records),
        out_shape=jax.ShapeDtypeStruct((records, layout_b.units * UNIT, LANES), BF),
        in_specs=[smem] + [vmem] * 6,
        out_specs=vmem,
        scratch_shapes=[
            pltpu.VMEM((records * frame, n_whole * LANES), F32),
            pltpu.VMEM((2, n_whole, wave.shape[0] // 2, LANES), F32),
        ],
        compiler_params=shared,
        name="second",
    )
    message_b = second(cable_depth, energy, odd, place, wave_kept, odd_kept, vertical_kept)
    arrived_b = lax.all_to_all(message_b, "shard", split_axis=0, concat_axis=0, tiled=True)

    if pairwise:
        packed = pl.pallas_call(
            repack_kernel(planes),
            out_shape=jax.ShapeDtypeStruct((planes, *sources[0].shape[1:]), BF),
            in_specs=[vmem] * planes,
            out_specs=vmem,
            compiler_params=shared,
            name="repack",
        )(*sources)
        sources.append(lax.ppermute(packed, "shard", [(s, s ^ 1) for s in range(records)]))

    forward = shot_forward(records, block)
    inverse = shot_inverse(records)
    response = response_table(records, n_samples, even_tiles + [mixed])
    even_inverse = np.ascontiguousarray(even_table.T)
    even, forward_b, mixed_part = pl.pallas_call(
        even_kernel(per, block, layout, records, len(sources)),
        out_shape=(
            jax.ShapeDtypeStruct((per * records, half), F32),
            jax.ShapeDtypeStruct(forward.shape, BF),
            jax.ShapeDtypeStruct((per * records, LANES), BF),
        ),
        in_specs=[smem] + [hbm] * 4 + [vmem] * len(sources),
        out_specs=(hbm,) * 3,
        scratch_shapes=[
            pltpu.VMEM((per * records, half), F32),
            scratch(forward),
            scratch(forward),
            scratch(forward),
            scratch(inverse),
            scratch(response),
            scratch(even_inverse),
            pltpu.VMEM((per * records, (n_whole + 1) * LANES), BF),
            pltpu.SemaphoreType.DMA((7,)),
        ],
        compiler_params=shared,
        name="even",
    )(shot_slot, forward, inverse, response, even_inverse, *sources)
    out = pl.pallas_call(
        last_kernel(per, block, layout_b, n_channels * records, records),
        out_shape=jax.ShapeDtypeStruct((per * records, n_samples), F32),
        in_specs=[hbm] * 7,
        out_specs=hbm,
        scratch_shapes=[
            scratch(arrived_b),
            scratch(forward),
            scratch(inverse),
            pltpu.VMEM((2 * records, n_whole * LANES), F32),
            scratch(odd_table.T),
            pltpu.VMEM((per * records, half), F32),
            pltpu.VMEM((per * records, (n_whole + 1) * LANES), BF),
            pltpu.VMEM((per * records, n_samples), F32),
            pltpu.SemaphoreType.DMA((6 + 3 * (half // 256),)),
        ],
        compiler_params=most,
        name="last",
    )(arrived_b, forward_b, inverse, response_table(records, n_samples, odd_tiles), mixed_part, np.ascontiguousarray(odd_table.T), even)
    return out.reshape(per, records, n_samples)


def solution(mesh):
    in_specs = (
        P(("groups", "shard"), None),
        P(("groups", "shard")),
        P(("groups", "shard")),
        P("groups"),
        P("groups"),
    )
    out_specs = P(("groups", "shard"), None, None)
    return jax.shard_map(shards, mesh=mesh, in_specs=in_specs, out_specs=out_specs, check_vma=False)
```

profile of v0, /device:TPU:9, one launch (start us, length us, event | category | flops | bytes accessed | tf_op | source)
XLA Modules:
  0.0 73.4 jit_solution(266895594769356349)
XLA Ops:
  0.7 9.4 %front.1 = (bf16[2,216,128]{2,1,0:T(8,128)(2,1)}, bf16[2,216,128]{2,1,0:T(8,128)(2,1)}, bf16[2,216,128]{2,1,0:T(8,128)(2,1)}, bf16[2,216,128]{2,1,0:T(8,128)(2,1...) custom-call(f32[1]{0:T(128)S(6)} %copy.18.depth_ref, ...), custom_call_target="tpu_custom_call" | custom-call | tf_op jit(solution)/shard_map/front/pallas_call | solution.py:486
  10.0 0.0 copy-start.15
  10.0 0.0 copy-start.14
  10.0 0.0 copy-start.13
  10.1 0.0 copy-start.12
  10.1 0.0 copy-start.11
  10.1 0.0 copy-start.10
  10.1 0.0 copy-start.9
  10.1 3.7 %second.1 = bf16[16,176,128]{2,1,0:T(8,128)(2,1)} custom-call(f32[1]{0:T(128)S(6)} %copy.18.depth_ref, f32[1,128]{1,0:T(1,128)S(1)} %get-tuple-element.22.energy_ref, bf16[648,1024]{1,0:T(8,128)(2,1)S(1)} %get-tuple-element.23.odd_ref, bf16[768,672]{1,0:T(8,128)(2,1)S(1)} %get-tuple-element.24.place_ref, bf16[672,648]{1,0:T(8,128)(2,1)S(1)} %get-tuple-element.25.wave_ref, ...), custom_call_target="tpu_custom_call" | custom-call | tf_op jit(solution)/shard_map/second/pallas_call | solution.py:531
  13.8 0.0 copy-start.2
  13.8 0.0 copy-start.1
  13.8 0.0 copy-start.3
  13.8 0.0 copy-start.4
  13.8 0.0 copy-start.5
  13.8 0.0 copy-start.7
  13.8 6.7 %all-to-all-start = ((bf16[16,176,128]{2,1,0:T(8,128)(2,1)}), bf16[16,176,128]{2,1,0:T(8,128)(2,1)S(1)}, u32[]{:S(2)}, u32[]{:S(2)}) async-start(bf16[16,176,128]{2,1,0:T(8,128)(2,1)} %second.1), calls=%async_computation | async-start | bytes 1441792 | tf_op jit(solution)/shard_map/all_to_all | solution.py:532
  20.5 0.0 copy-done.15
  20.5 1.2 %collective-permute-start = (bf16[2,216,128]{2,1,0:T(8,128)(2,1)S(1)}, bf16[2,216,128]{2,1,0:T(8,128)(2,1)S(1)}, u32[]{:S(2)}, u32[]{:S(2)}) collective-permute-start(bf16[2,216,128]{2,1,0:T(8,128)(2,1)S(1)} %copy-done.15), channel_id=1, source_target_pairs={{0,2},{1,3},{2,0},{3,1},{4,6},{5,7},{6,4},{7,5},{8,10},{9,11},{10,... | collective-permute-start | bytes 331784 | tf_op jit(solution)/shard_map/ppermute | solution.py:515
  21.8 0.0 copy-done.14
  21.8 1.2 %collective-permute-start.1 = (bf16[2,216,128]{2,1,0:T(8,128)(2,1)S(1)}, bf16[2,216,128]{2,1,0:T(8,128)(2,1)S(1)}, u32[]{:S(2)}, u32[]{:S(2)}) collective-permute-start(bf16[2,216,128]{2,1,0:T(8,128)(2,1)S(1)} %copy-done.14), channel_id=1, source_target_pairs={{0,4},{1,5},{2,6},{3,7},{4,8},{5,9},{6,10},{7,11},{8,12},{9,13},{1... | collective-permute-start | bytes 331784 | tf_op jit(solution)/shard_map/ppermute | solution.py:515
  22.9 0.0 copy-done.13
  22.9 1.2 %collective-permute-start.2 = (bf16[2,216,128]{2,1,0:T(8,128)(2,1)S(1)}, bf16[2,216,128]{2,1,0:T(8,128)(2,1)S(1)}, u32[]{:S(2)}, u32[]{:S(2)}) collective-permute-start(bf16[2,216,128]{2,1,0:T(8,128)(2,1)S(1)} %copy-done.13), channel_id=1, source_target_pairs={{0,6},{1,7},{2,4},{3,5},{4,10},{5,11},{6,8},{7,9},{8,14},{9,15},{1... | collective-permute-start | bytes 331784 | tf_op jit(solution)/shard_map/ppermute | solution.py:515
  24.1 0.0 copy-done.12
  24.1 1.2 %collective-permute-start.3 = (bf16[2,216,128]{2,1,0:T(8,128)(2,1)S(1)}, bf16[2,216,128]{2,1,0:T(8,128)(2,1)S(1)}, u32[]{:S(2)}, u32[]{:S(2)}) collective-permute-start(bf16[2,216,128]{2,1,0:T(8,128)(2,1)S(1)} %copy-done.12), channel_id=1, source_target_pairs={{0,8},{1,9},{2,10},{3,11},{4,12},{5,13},{6,14},{7,15},{8,0},{9,1},... | collective-permute-start | bytes 331784 | tf_op jit(solution)/shard_map/ppermute | solution.py:515
  25.3 0.0 copy-done.11
  25.3 2.1 %collective-permute-start.4 = (bf16[2,216,128]{2,1,0:T(8,128)(2,1)S(1)}, bf16[2,216,128]{2,1,0:T(8,128)(2,1)S(1)}, u32[]{:S(2)}, u32[]{:S(2)}) collective-permute-start(bf16[2,216,128]{2,1,0:T(8,128)(2,1)S(1)} %copy-done.11), channel_id=1, source_target_pairs={{0,10},{1,11},{2,8},{3,9},{4,14},{5,15},{6,12},{7,13},{8,2},{9,3},... | collective-permute-start | bytes 331784 | tf_op jit(solution)/shard_map/ppermute | solution.py:515
  27.4 0.9 %collective-permute-done.refs_1_ = bf16[2,216,128]{2,1,0:T(8,128)(2,1)S(1)} collective-permute-done((bf16[2,216,128]{2,1,0:T(8,128)(2,1)S(1)}, bf16[2,216,128]{2,1,0:T(8,128)(2,1)S(1)}, u32[]{:S(2)}, u32[]{:S(2)}) %collective-permute-start) | collective-permute-done | bytes 110624 | tf_op jit(solution)/shard_map/ppermute | solution.py:515
  28.3 0.0 copy-done.10
  28.3 1.5 %collective-permute-start.5 = (bf16[2,216,128]{2,1,0:T(8,128)(2,1)S(1)}, bf16[2,216,128]{2,1,0:T(8,128)(2,1)S(1)}, u32[]{:S(2)}, u32[]{:S(2)}) collective-permute-start(bf16[2,216,128]{2,1,0:T(8,128)(2,1)S(1)} %copy-done.10), channel_id=1, source_target_pairs={{0,12},{1,13},{2,14},{3,15},{4,0},{5,1},{6,2},{7,3},{8,4},{9,5},{1... | collective-permute-start | bytes 331784 | tf_op jit(solution)/shard_map/ppermute | solution.py:515
  29.8 18.2 %collective-permute-done.1.refs_2_ = bf16[2,216,128]{2,1,0:T(8,128)(2,1)S(1)} collective-permute-done((bf16[2,216,128]{2,1,0:T(8,128)(2,1)S(1)}, bf16[2,216,128]{2,1,0:T(8,128)(2,1)S(1)}, u32[]{:S(2)}, u32[]{:S(2)}) %collective-permute-start.1) | collective-permute-done | bytes 110624 | tf_op jit(solution)/shard_map/ppermute | solution.py:515
  48.0 0.0 copy-done.9
  48.0 0.0 collective-permute-start.6
  48.0 2.4 %collective-permute-done.2.refs_3_ = bf16[2,216,128]{2,1,0:T(8,128)(2,1)S(1)} collective-permute-done((bf16[2,216,128]{2,1,0:T(8,128)(2,1)S(1)}, bf16[2,216,128]{2,1,0:T(8,128)(2,1)S(1)}, u32[]{:S(2)}, u32[]{:S(2)}) %collective-permute-start.2) | collective-permute-done | bytes 110624 | tf_op jit(solution)/shard_map/ppermute | solution.py:515
  50.4 2.4 %collective-permute-done.3.refs_4_ = bf16[2,216,128]{2,1,0:T(8,128)(2,1)S(1)} collective-permute-done((bf16[2,216,128]{2,1,0:T(8,128)(2,1)S(1)}, bf16[2,216,128]{2,1,0:T(8,128)(2,1)S(1)}, u32[]{:S(2)}, u32[]{:S(2)}) %collective-permute-start.3) | collective-permute-done | bytes 110624 | tf_op jit(solution)/shard_map/ppermute | solution.py:515
  52.8 2.4 %collective-permute-done.4.refs_5_ = bf16[2,216,128]{2,1,0:T(8,128)(2,1)S(1)} collective-permute-done((bf16[2,216,128]{2,1,0:T(8,128)(2,1)S(1)}, bf16[2,216,128]{2,1,0:T(8,128)(2,1)S(1)}, u32[]{:S(2)}, u32[]{:S(2)}) %collective-permute-start.4) | collective-permute-done | bytes 110624 | tf_op jit(solution)/shard_map/ppermute | solution.py:515
  55.1 0.0 collective-permute-done.5.refs_6_
  55.1 2.8 %collective-permute-done.6.refs_7_ = bf16[2,216,128]{2,1,0:T(8,128)(2,1)S(1)} collective-permute-done((bf16[2,216,128]{2,1,0:T(8,128)(2,1)S(1)}, bf16[2,216,128]{2,1,0:T(8,128)(2,1)S(1)}, u32[]{:S(2)}, u32[]{:S(2)}) %collective-permute-start.6) | collective-permute-done | bytes 110624 | tf_op jit(solution)/shard_map/ppermute | solution.py:515
  58.0 0.0 copy-done.2
  58.0 0.0 copy-start.6
  58.0 1.0 %collective-permute-start.7 = (bf16[8,216,128]{2,1,0:T(8,128)(2,1)S(1)}, bf16[8,216,128]{2,1,0:T(8,128)(2,1)S(1)}, u32[]{:S(2)}, u32[]{:S(2)}) collective-permute-start(bf16[8,216,128]{2,1,0:T(8,128)(2,1)S(1)} %repack.1), channel_id=1, source_target_pairs={{0,1},{1,0},{2,3},{3,2},{4,5},{5,4},{6,7},{7,6},{8,9},{9,8},{10,11... | collective-permute-start | bytes 1327112 | tf_op jit(solution)/shard_map/ppermute | solution.py:543
  59.0 1.4 %collective-permute-done.7.refs_8_ = bf16[8,216,128]{2,1,0:T(8,128)(2,1)S(1)} collective-permute-done((bf16[8,216,128]{2,1,0:T(8,128)(2,1)S(1)}, bf16[8,216,128]{2,1,0:T(8,128)(2,1)S(1)}, u32[]{:S(2)}, u32[]{:S(2)}) %collective-permute-start.7) | collective-permute-done | bytes 442400 | tf_op jit(solution)/shard_map/ppermute | solution.py:543
  60.5 0.0 copy-done.1
  60.5 0.0 copy-done.3
  60.5 0.0 copy-done.4
  60.5 0.0 copy-done.5
  60.5 0.0 copy-done.7
  60.5 4.2 %even.1 = (f32[672,1024]{1,0:T(8,128)S(1)}, bf16[512,256]{1,0:T(8,128)(2,1)S(1)}, bf16[672,128]{1,0:T(8,128)(2,1)S(1)}) custom-call(s32[16]{0:T(128)S(1)} %copy-done.7, bf16[512,256]{1,0:T(8,128)(2,1)S(1)} %copy-done.4, bf16[128,256]{1,0:T(8,128)(2,1)S(1)} %copy-done.3, f32[32,640]{1,0:T(8,128)S(1)} %copy-done.5, bf16[640,1024]{1,0:T(8,128)(2,1)S(1)} %copy-done.1, ...), custom_call_target="tpu_custom_call" | custom-call | tf_op jit(solution)/shard_map/even/pallas_call | solution.py:549
  64.7 0.0 copy-start
  64.7 1.5 %copy-done = f32[672,1024]{1,0:T(8,128)} copy-done((f32[672,1024]{1,0:T(8,128)}, f32[672,1024]{1,0:T(8,128)S(1)}, u32[]{:S(2)}) %copy-start) | copy-done | bytes 2752536
  66.3 0.0 all-to-all-done.arrived_hbm
  66.3 0.0 copy-start.8
  66.3 0.9 %copy-done.8 = bf16[16,176,128]{2,1,0:T(8,128)(2,1)} copy-done((bf16[16,176,128]{2,1,0:T(8,128)(2,1)}, bf16[16,176,128]{2,1,0:T(8,128)(2,1)S(1)}, u32[]{:S(2)}) %copy-start.8) | copy-done | bytes 720920
  67.1 0.0 copy-done.6
  67.1 6.1 %last.1 = f32[672,2048]{1,0:T(8,128)} custom-call(bf16[16,176,128]{2,1,0:T(8,128)(2,1)} %copy-done.8, bf16[512,256]{1,0:T(8,128)(2,1)S(1)} %get-tuple-element.36.forward_hbm, bf16[128,256]{1,0:T(8,128)(2,1)S(1)} %copy-done.3, f32[32,512]{1,0:T(8,128)S(1)} %copy-done.6, bf16[672,128]{1,0:T(8,128)(2,1)S(1)} %get-tuple-element.37.mixed_hbm, ...), custom_call_target="tpu_custom_call" | custom-call | tf_op jit(solution)/shard_map/last/pallas_call | solution.py:572
  (1 shorter events, 0.0 us)
Async XLA Ops:
  10.0 10.5 %copy-start.15 = (bf16[2,216,128]{2,1,0:T(8,128)(2,1)S(1)}, bf16[2,216,128]{2,1,0:T(8,128)(2,1)}, u32[]{:S(2)}) copy-start(bf16[2,216,128]{2,1,0:T(8,128)(2,1)} %get-tuple-element.29) | copy-start | bytes 331780
  10.0 11.7 %copy-start.14 = (bf16[2,216,128]{2,1,0:T(8,128)(2,1)S(1)}, bf16[2,216,128]{2,1,0:T(8,128)(2,1)}, u32[]{:S(2)}) copy-start(bf16[2,216,128]{2,1,0:T(8,128)(2,1)} %get-tuple-element.30) | copy-start | bytes 331780
  10.0 12.9 %copy-start.13 = (bf16[2,216,128]{2,1,0:T(8,128)(2,1)S(1)}, bf16[2,216,128]{2,1,0:T(8,128)(2,1)}, u32[]{:S(2)}) copy-start(bf16[2,216,128]{2,1,0:T(8,128)(2,1)} %get-tuple-element.31) | copy-start | bytes 331780
  10.1 14.1 %copy-start.12 = (bf16[2,216,128]{2,1,0:T(8,128)(2,1)S(1)}, bf16[2,216,128]{2,1,0:T(8,128)(2,1)}, u32[]{:S(2)}) copy-start(bf16[2,216,128]{2,1,0:T(8,128)(2,1)} %get-tuple-element.32) | copy-start | bytes 331780
  10.1 15.3 %copy-start.11 = (bf16[2,216,128]{2,1,0:T(8,128)(2,1)S(1)}, bf16[2,216,128]{2,1,0:T(8,128)(2,1)}, u32[]{:S(2)}) copy-start(bf16[2,216,128]{2,1,0:T(8,128)(2,1)} %get-tuple-element.33) | copy-start | bytes 331780
  10.1 18.3 %copy-start.10 = (bf16[2,216,128]{2,1,0:T(8,128)(2,1)S(1)}, bf16[2,216,128]{2,1,0:T(8,128)(2,1)}, u32[]{:S(2)}) copy-start(bf16[2,216,128]{2,1,0:T(8,128)(2,1)} %get-tuple-element.34) | copy-start | bytes 331780
  10.1 37.9 %copy-start.9 = (bf16[2,216,128]{2,1,0:T(8,128)(2,1)S(1)}, bf16[2,216,128]{2,1,0:T(8,128)(2,1)}, u32[]{:S(2)}) copy-start(bf16[2,216,128]{2,1,0:T(8,128)(2,1)} %get-tuple-element.35) | copy-start | bytes 331780
  13.8 44.2 %copy-start.2 = (bf16[2,216,128]{2,1,0:T(8,128)(2,1)S(1)}, bf16[2,216,128]{2,1,0:T(8,128)(2,1)}, u32[]{:S(2)}) copy-start(bf16[2,216,128]{2,1,0:T(8,128)(2,1)} %get-tuple-element.28.refs_0_) | copy-start | bytes 331780
  13.8 46.7 %copy-start.1 = (bf16[640,1024]{1,0:T(8,128)(2,1)S(1)}, bf16[640,1024]{1,0:T(8,128)(2,1)}, u32[]{:S(2)}) copy-start(bf16[640,1024]{1,0:T(8,128)(2,1)} %constant.33.clone.table_hbm) | copy-start | bytes 3932164
  13.8 46.7 %copy-start.3 = (bf16[128,256]{1,0:T(8,128)(2,1)S(1)}, bf16[128,256]{1,0:T(8,128)(2,1)}, u32[]{:S(2)}) copy-start(bf16[128,256]{1,0:T(8,128)(2,1)} %constant.31.clone.inverse_hbm) | copy-start | bytes 196612
  13.8 46.7 %copy-start.4 = (bf16[512,256]{1,0:T(8,128)(2,1)S(1)}, bf16[512,256]{1,0:T(8,128)(2,1)}, u32[]{:S(2)}) copy-start(bf16[512,256]{1,0:T(8,128)(2,1)} %constant.30.clone.forward_hbm) | copy-start | bytes 786436
  13.8 46.7 %copy-start.5 = (f32[32,640]{1,0:T(8,128)S(1)}, f32[32,640]{1,0:T(8,128)}, u32[]{:S(2)}) copy-start(f32[32,640]{1,0:T(8,128)} %constant.32.clone.response_hbm) | copy-start | bytes 245764
  13.8 46.7 %copy-start.7 = (s32[16]{0:T(128)S(1)}, s32[16]{0:T(128)}, u32[]{:S(2)}) copy-start(s32[16]{0:T(128)} %slot_ref.1) | copy-start | bytes 196
  13.8 52.5 %all-to-all-start = ((bf16[16,176,128]{2,1,0:T(8,128)(2,1)}), bf16[16,176,128]{2,1,0:T(8,128)(2,1)S(1)}, u32[]{:S(2)}, u32[]{:S(2)}) async-start(bf16[16,176,128]{2,1,0:T(8,128)(2,1)} %second.1), calls=%async_computation | async-start | bytes 1441792 | tf_op jit(solution)/shard_map/all_to_all | solution.py:532
  20.5 7.8 %collective-permute-start = (bf16[2,216,128]{2,1,0:T(8,128)(2,1)S(1)}, bf16[2,216,128]{2,1,0:T(8,128)(2,1)S(1)}, u32[]{:S(2)}, u32[]{:S(2)}) collective-permute-start(bf16[2,216,128]{2,1,0:T(8,128)(2,1)S(1)} %copy-done.15), channel_id=1, source_target_pairs={{0,2},{1,3},{2,0},{3,1},{4,6},{5,7},{6,4},{7,5},{8,10},{9,11},{10,... | collective-permute-start | bytes 331784 | tf_op jit(solution)/shard_map/ppermute | solution.py:515
  21.8 26.3 %collective-permute-start.1 = (bf16[2,216,128]{2,1,0:T(8,128)(2,1)S(1)}, bf16[2,216,128]{2,1,0:T(8,128)(2,1)S(1)}, u32[]{:S(2)}, u32[]{:S(2)}) collective-permute-start(bf16[2,216,128]{2,1,0:T(8,128)(2,1)S(1)} %copy-done.14), channel_id=1, source_target_pairs={{0,4},{1,5},{2,6},{3,7},{4,8},{5,9},{6,10},{7,11},{8,12},{9,13},{1... | collective-permute-start | bytes 331784 | tf_op jit(solution)/shard_map/ppermute | solution.py:515
  22.9 27.4 %collective-permute-start.2 = (bf16[2,216,128]{2,1,0:T(8,128)(2,1)S(1)}, bf16[2,216,128]{2,1,0:T(8,128)(2,1)S(1)}, u32[]{:S(2)}, u32[]{:S(2)}) collective-permute-start(bf16[2,216,128]{2,1,0:T(8,128)(2,1)S(1)} %copy-done.13), channel_id=1, source_target_pairs={{0,6},{1,7},{2,4},{3,5},{4,10},{5,11},{6,8},{7,9},{8,14},{9,15},{1... | collective-permute-start | bytes 331784 | tf_op jit(solution)/shard_map/ppermute | solution.py:515
  24.1 28.6 %collective-permute-start.3 = (bf16[2,216,128]{2,1,0:T(8,128)(2,1)S(1)}, bf16[2,216,128]{2,1,0:T(8,128)(2,1)S(1)}, u32[]{:S(2)}, u32[]{:S(2)}) collective-permute-start(bf16[2,216,128]{2,1,0:T(8,128)(2,1)S(1)} %copy-done.12), channel_id=1, source_target_pairs={{0,8},{1,9},{2,10},{3,11},{4,12},{5,13},{6,14},{7,15},{8,0},{9,1},... | collective-permute-start | bytes 331784 | tf_op jit(solution)/shard_map/ppermute | solution.py:515
  25.3 29.8 %collective-permute-start.4 = (bf16[2,216,128]{2,1,0:T(8,128)(2,1)S(1)}, bf16[2,216,128]{2,1,0:T(8,128)(2,1)S(1)}, u32[]{:S(2)}, u32[]{:S(2)}) collective-permute-start(bf16[2,216,128]{2,1,0:T(8,128)(2,1)S(1)} %copy-done.11), channel_id=1, source_target_pairs={{0,10},{1,11},{2,8},{3,9},{4,14},{5,15},{6,12},{7,13},{8,2},{9,3},... | collective-permute-start | bytes 331784 | tf_op jit(solution)/shard_map/ppermute | solution.py:515
  28.3 26.8 %collective-permute-start.5 = (bf16[2,216,128]{2,1,0:T(8,128)(2,1)S(1)}, bf16[2,216,128]{2,1,0:T(8,128)(2,1)S(1)}, u32[]{:S(2)}, u32[]{:S(2)}) collective-permute-start(bf16[2,216,128]{2,1,0:T(8,128)(2,1)S(1)} %copy-done.10), channel_id=1, source_target_pairs={{0,12},{1,13},{2,14},{3,15},{4,0},{5,1},{6,2},{7,3},{8,4},{9,5},{1... | collective-permute-start | bytes 331784 | tf_op jit(solution)/shard_map/ppermute | solution.py:515
  48.0 9.9 %collective-permute-start.6 = (bf16[2,216,128]{2,1,0:T(8,128)(2,1)S(1)}, bf16[2,216,128]{2,1,0:T(8,128)(2,1)S(1)}, u32[]{:S(2)}, u32[]{:S(2)}) collective-permute-start(bf16[2,216,128]{2,1,0:T(8,128)(2,1)S(1)} %copy-done.9), channel_id=1, source_target_pairs={{0,14},{1,15},{2,12},{3,13},{4,2},{5,3},{6,0},{7,1},{8,6},{9,7},{1... | collective-permute-start | bytes 331784 | tf_op jit(solution)/shard_map/ppermute | solution.py:515
  58.0 9.1 %copy-start.6 = (f32[32,512]{1,0:T(8,128)S(1)}, f32[32,512]{1,0:T(8,128)}, u32[]{:S(2)}) copy-start(f32[32,512]{1,0:T(8,128)} %constant.34.clone.response_hbm) | copy-start | bytes 196612
  58.0 2.5 %collective-permute-start.7 = (bf16[8,216,128]{2,1,0:T(8,128)(2,1)S(1)}, bf16[8,216,128]{2,1,0:T(8,128)(2,1)S(1)}, u32[]{:S(2)}, u32[]{:S(2)}) collective-permute-start(bf16[8,216,128]{2,1,0:T(8,128)(2,1)S(1)} %repack.1), channel_id=1, source_target_pairs={{0,1},{1,0},{2,3},{3,2},{4,5},{5,4},{6,7},{7,6},{8,9},{9,8},{10,11... | collective-permute-start | bytes 1327112 | tf_op jit(solution)/shard_map/ppermute | solution.py:543
  64.7 1.5 %copy-start = (f32[672,1024]{1,0:T(8,128)}, f32[672,1024]{1,0:T(8,128)S(1)}, u32[]{:S(2)}) copy-start(f32[672,1024]{1,0:T(8,128)S(1)} %get-tuple-element.38.even_hbm) | copy-start | bytes 8257540
  66.3 0.9 %copy-start.8 = (bf16[16,176,128]{2,1,0:T(8,128)(2,1)}, bf16[16,176,128]{2,1,0:T(8,128)(2,1)S(1)}, u32[]{:S(2)}) copy-start(bf16[16,176,128]{2,1,0:T(8,128)(2,1)S(1)} %all-to-all-done.arrived_hbm) | copy-start | bytes 2162692
where the time goes:
time: 73.7 us; the launch traced here: 73.4 us
  waiting for transfers between devices  30.5 us (41%)
  Pallas kernels  23.4 us (32%)
  starting transfers between devices  16.1 us (22%)
  local copies, waits for them, and re-layouts  2.45 us (3%)
  between operations  0.96 us (1%)
    ppermute x7, waiting for transfers between devices, shards(): sources[chip] = lax.ppermute(sources[chip], 'shard', route)  29.1 us
    pallas_call x1, Pallas kernels, shards(): pl.pallas_call(front_kernel(per, frame, layout, records, planes), out_sha...  9.36 us
    ppermute x7, starting transfers between devices, shards(): sources[chip] = lax.ppermute(sources[chip], 'shard', route)  8.36 us
    all_to_all x1, starting transfers between devices, shards(): lax.all_to_all(message_b, 'shard', split_axis=0, concat_axis=0, tiled=True)  6.7 us
    pallas_call x1, Pallas kernels, shards(): pl.pallas_call(last_kernel(per, block, layout_b, n_channels * records, re...  6.15 us
    pallas_call x1, Pallas kernels, shards(): pl.pallas_call(even_kernel(per, block, layout, records, len(sources)), ou...  4.23 us
    pallas_call x1, Pallas kernels, shards(): second(cable_depth, energy, odd, place, wave_kept, odd_kept, vertical_kept)  3.68 us
    unnamed x32, local copies, waits for them, and re-layouts  2.45 us
  transfers between devices with their start and end apart: 9, of which 7 were waited for; matrix products, arithmetic and copies ran while one was open for 0% of the time, Pallas kernels for 6%

commit v1 on v0

--- a/solution.py
+++ b/solution.py
@@ -27,6 +27,7 @@
 LANES = 128
 HALF = 64
 UNIT = 8
+STRIP = 512
 ALL_VMEM = 60 << 20
 MOST_VMEM = 53 << 20
 FRONT_VMEM = 52 << 20
@@ -79,7 +80,7 @@
     kx = 2.0 * np.pi * k / (n_channels * channel_spacing)
     bins = np.concatenate(tiles).astype(np.float64)
     slow = 2.0 * np.pi * bins / (n_samples * sample_step) / water_speed
-    return (2.0 * np.sqrt(np.maximum(slow[None, :] ** 2 - kx[:, None] ** 2, 0.0))).astype(np.float32)
+    return np.sqrt(np.maximum(slow[None, :] ** 2 - kx[:, None] ** 2, 0.0)).astype(np.float32)
 
 
 def shot_basis(records):
@@ -117,25 +118,30 @@
 
 
 def sin_cos(angle):
-    turns = jnp.floor(angle * (2.0 / math.pi) + 0.5)
-    rest = ((angle - turns * 1.5703125) - turns * 4.837512969970703125e-4) - turns * 7.54978995489188216e-8
+    turns = jnp.floor(angle * (1.0 / math.pi) + 0.5)
+    rest = ((angle - turns * 3.140625) - turns * 9.67502593994140625e-4) - turns * 1.509957990978376432e-7
     sq = rest * rest
-    sine = ((-1.9515295891e-4 * sq + 8.3321608736e-3) * sq - 1.6666654611e-1) * sq * rest + rest
-    cosine = ((2.443315711809948e-5 * sq - 1.388731625493765e-3) * sq + 4.166664568298827e-2) * sq * sq - 0.5 * sq + 1.0
-    quarter = turns.astype(jnp.int32)
-    odd = (quarter & 1) == 1
-    sin_out = jnp.where(odd, cosine, sine)
-    cos_out = jnp.where(odd, sine, cosine)
-    sin_out = jnp.where((quarter & 2) == 2, -sin_out, sin_out)
-    cos_out = jnp.where(((quarter + 1) & 2) == 2, -cos_out, cos_out)
-    return sin_out, cos_out
+    sine = -2.3889859e-8 * sq + 2.7525562e-6
+    sine = sine * sq - 1.9840874e-4
+    sine = sine * sq + 8.3333310e-3
+    sine = sine * sq - 1.6666667e-1
+    sine = sine * sq * rest + rest
+    cosine = -2.605e-7 * sq + 2.47609e-5
+    cosine = cosine * sq - 1.3888397e-3
+    cosine = cosine * sq + 4.16666418e-2
+    cosine = cosine * sq - 0.4999999963
+    cosine = cosine * sq + 1.0
+    return sine, cosine
 
 
 def gains(vertical, depth, weight):
     sine, cosine = sin_cos(vertical * depth)
-    denominator = 1.0 - 2.0 * surface_reflect * cosine + surface_reflect * surface_reflect + ghost_floor
-    scale = weight / denominator
-    return (1.0 - surface_reflect * cosine) * scale, -surface_reflect * sine * scale
+    double = 2.0 * sine
+    less = sine * double
+    top = 1.0 - surface_reflect
+    bottom = 1.0 - 2.0 * surface_reflect + surface_reflect * surface_reflect + ghost_floor
+    scale = weight / (bottom + 2.0 * surface_reflect * less)
+    return (top + surface_reflect * less) * scale, (-surface_reflect * double) * cosine * scale
 
 
 def tile_gains(gain_re, gain_im, second):
@@ -167,12 +173,12 @@
     return join(lifted)
 
 
-def store_factors(factors_ref, vertical_ref, depth, n_channels):
+def store_factors(factors_ref, vertical_ref, depth, n_channels, first=None):
     tiles = factors_ref.shape[1]
     row = lax.broadcasted_iota(jnp.int32, (vertical_ref.shape[0], LANES), 0)
     single = (row == 0) | (row * 2 == n_channels)
     weight = jnp.where(single, 1.0 / n_channels, 2.0 / n_channels)
-    for t in range(0, tiles, 2):
+    for t in range(0, tiles, 2) if first is None else (first,):
         gain_re, gain_im = gains(vertical_ref[:, t * HALF : (t + 2) * HALF], depth, weight)
         for h in range(min(2, tiles - t)):
             factors_ref[0, t + h], factors_ref[1, t + h] = tile_gains(gain_re, gain_im, h == 1)
@@ -213,7 +219,7 @@
 
 def chips(records):
     n = records // 4
-    far = sorted(range(1, n), key=lambda d: -min(d, n - d))
+    far = sorted(range(1, n), key=lambda d: min(d, n - d))
     return [2 * dz + dx for dz in far for dx in range(2)] + [1]
 
 
@@ -290,7 +296,6 @@
         copies[0].wait()
         copies[1].wait()
         place_ref[...] = lax.dot_general(picked, wave_ref[...], (((1,), (1,)), ((), ())), preferred_element_type=F32).astype(BF)
-        store_factors(factors_ref, vertical_ref, depth_ref[0], n_channels)
         outs = start_all(list(zip(later_hbm, later)), sems, len(copies))
         for s in range(steps):
             copies[2 + s].wait()
@@ -299,12 +304,17 @@
             second = traces_ref[part, half:]
             sum_ref[part, :] = (first + second).astype(BF)
             odd_ref[part, :] = (first - second).astype(BF)
-        copies[-2].wait()
-        even = dot(sum_ref[...], table_ref[...])
-        copies[-1].wait()
-        whole = (layout.tiles - 1) * LANES
-        mixed = even[:, whole:] + dot(odd_ref[...], mixed_ref[...])
-        spec = jnp.concatenate([even[:, :whole].astype(BF), mixed.astype(BF)], axis=1)
+        for c in copies[-2:]:
+            c.wait()
+        spec = []
+        for t in range(0, layout.tiles, 2):
+            cols = slice(t * LANES, min(t + 2, layout.tiles) * LANES)
+            got = dot(sum_ref[...], table_ref[:, cols])
+            if t + 2 > layout.tiles:
+                got = got + dot(odd_ref[...], mixed_ref[...])
+            spec.append(got.astype(BF))
+            store_factors(factors_ref, vertical_ref, depth_ref[0], n_channels, t)
+        spec = jnp.concatenate(spec, axis=1)
         placed_ref[...] = dot(place_ref[...], lift(spec, factors_ref, 0, wave_ref))
         energy_ref[...] = energy_of(placed_ref[...])
         for i in range(records):
@@ -340,12 +350,12 @@
     return jnp.where(lax.broadcasted_iota(jnp.int32, (size, size), 0) == goal, 1.0, 0.0).astype(BF)
 
 
-def filter_gathers(arrived, layout, forward_ref, inverse_ref, response_ref, out_ref, per, block):
+def filter_gathers(arrived, layout, forward_ref, inverse_ref, response_ref, out_ref, per, block, blocks=None):
     k = response_ref.shape[0]
     records = k // 2
     blank = jnp.zeros((UNIT, LANES), F32)
     units = [a.astype(F32) for a in arrived]
-    for b in range(-(-per // block)):
+    for b in range(-(-per // block)) if blocks is None else blocks:
         live = min(block, per - b * block)
         sides = []
         for t in range(layout.tiles):
@@ -414,12 +424,12 @@
     def kernel(arrived_hbm, forward_hbm, inverse_hbm, response_hbm, mixed_hbm, odd_table_hbm, even_hbm,
                out_hbm, arrived_ref, forward_ref, inverse_ref, response_ref, odd_table_ref, even_ref, filtered_ref, out_ref, sems):
         half = even_ref.shape[1]
-        strip = 256
-        cuts = [pl.ds(s, strip) for s in range(0, half, strip)]
+        strip = STRIP
+        cuts = [pl.ds(g * records, min(block, per - g) * records) for g in range(0, per, block)]
         mixed = filtered_ref.at[:, pl.ds(layout.tiles * LANES, LANES)]
         first = [(arrived_hbm, arrived_ref), (forward_hbm, forward_ref), (inverse_hbm, inverse_ref), (response_hbm, response_ref)]
         fetch = start_all(first + [(odd_table_hbm, odd_table_ref), (mixed_hbm, mixed)], sems)
-        fetch += start_all([(even_hbm.at[:, c], even_ref.at[:, c]) for c in cuts], sems, len(fetch))
+        fetch += start_all([(even_hbm.at[c, :], even_ref.at[c, :]) for c in cuts], sems, len(fetch))
         for c in fetch[:4]:
             c.wait()
         arrived = [arrived_ref[s] for s in range(records)]
@@ -429,20 +439,24 @@
         ends = jnp.where((row == UNIT - 1) & (lane < 3), ends, 0.0)
         energy = jnp.sum(ends, keepdims=True)
         scale = lax.rsqrt(2.0 * FREQ * (energy * (1.0 / (n_traces * FREQ)) + energy_eps))
-        filter_gathers(arrived, layout, forward_ref, inverse_ref, response_ref, filtered_ref, per, block)
-        for c in fetch[4:6]:
-            c.wait()
         copies = []
-        for s in range(0, half, strip):
-            fetch[6 + s // strip].wait()
-            odd = dot(filtered_ref[...], odd_table_ref[:, s : s + strip])
-            even = even_ref[:, s : s + strip]
-            out_ref[:, s : s + strip] = (even + odd) * scale
-            out_ref[:, half + s : half + s + strip] = (even - odd) * scale
-            pairs = []
-            for here in (pl.ds(s, strip), pl.ds(half + s, strip)):
-                pairs.append((out_ref.at[:, here], out_hbm.at[:, here]))
-            copies += start_all(pairs, sems, len(fetch) + len(copies))
+        for b in range(len(cuts)):
+            filter_gathers(arrived, layout, forward_ref, inverse_ref, response_ref, filtered_ref, per, block, (b,))
+            if b == 0:
+                for c in fetch[4:6]:
+                    c.wait()
+            fetch[6 + b].wait()
+            here = cuts[b]
+            for s in range(0, half, strip):
+                cols = slice(s, s + strip)
+                odd = dot(filtered_ref[here, :], odd_table_ref[:, cols])
+                even = even_ref[here, cols]
+                out_ref[here, cols] = (even + odd) * scale
+                out_ref[here, half + s : half + s + strip] = (even - odd) * scale
+                pairs = []
+                for there in (pl.ds(s, strip), pl.ds(half + s, strip)):
+                    pairs.append((out_ref.at[here, there], out_hbm.at[here, there]))
+                copies += start_all(pairs, sems, len(fetch) + len(copies))
         for c in copies:
             c.wait()
 
@@ -583,7 +597,7 @@
             pltpu.VMEM((per * records, half), F32),
             pltpu.VMEM((per * records, (n_whole + 1) * LANES), BF),
             pltpu.VMEM((per * records, n_samples), F32),
-            pltpu.SemaphoreType.DMA((6 + 3 * (half // 256),)),
+            pltpu.SemaphoreType.DMA((6 + -(-per // block) * (1 + 2 * (half // STRIP)),)),
         ],
         compiler_params=most,
         name="last",

time: 73.7 us -> 72 us (0.977)
  Pallas kernels: 23.4 us -> 21.8 us
    pallas_call x1, Pallas kernels: 6.15 us -> 5.16 us  [shards(): pl.pallas_call(last_kernel(per, block, layout_b, n_channels * records, re...]
where the time goes in v1:
time: 72 us; the launch traced here: 71.8 us
  waiting for transfers between devices  30.5 us (42%)
  Pallas kernels  21.8 us (30%)
  starting transfers between devices  16.1 us (22%)
  local copies, waits for them, and re-layouts  2.45 us (3%)
  between operations  0.96 us (1%)
    ppermute x7, waiting for transfers between devices, shards(): sources[chip] = lax.ppermute(sources[chip], 'shard', route)  29.1 us
    pallas_call x1, Pallas kernels, shards(): pl.pallas_call(front_kernel(per, frame, layout, records, planes), out_sha...  8.83 us
    ppermute x7, starting transfers between devices, shards(): sources[chip] = lax.ppermute(sources[chip], 'shard', route)  8.36 us
    all_to_all x1, starting transfers between devices, shards(): lax.all_to_all(message_b, 'shard', split_axis=0, concat_axis=0, tiled=True)  6.69 us
    pallas_call x1, Pallas kernels, shards(): pl.pallas_call(last_kernel(per, block, layout_b, n_channels * records, re...  5.16 us
    pallas_call x1, Pallas kernels, shards(): pl.pallas_call(even_kernel(per, block, layout, records, len(sources)), ou...  4.23 us
    pallas_call x1, Pallas kernels, shards(): second(cable_depth, energy, odd, place, wave_kept, odd_kept, vertical_kept)  3.53 us
    unnamed x32, local copies, waits for them, and re-layouts  2.45 us
  transfers between devices with their start and end apart: 9, of which 7 were waited for; matrix products, arithmetic and copies ran while one was open for 0% of the time, Pallas kernels for 6%

profile of v1, /device:TPU:9, one launch (start us, length us, event | category | flops | bytes accessed | tf_op | source)
XLA Modules:
  0.0 71.8 jit_solution(4257332490834896083)
XLA Ops:
  0.7 8.8 %front.1 = (bf16[2,216,128]{2,1,0:T(8,128)(2,1)}, bf16[2,216,128]{2,1,0:T(8,128)(2,1)}, bf16[2,216,128]{2,1,0:T(8,128)(2,1)}, bf16[2,216,128]{2,1,0:T(8,128)(2,1...) custom-call(f32[1]{0:T(128)S(6)} %copy.18.depth_ref, ...), custom_call_target="tpu_custom_call" | custom-call | tf_op jit(solution)/shard_map/front/pallas_call | solution.py:500
  9.5 0.0 copy-start.15
  9.5 0.0 copy-start.14
  9.5 0.0 copy-start.13
  9.5 0.0 copy-start.12
  9.5 0.0 copy-start.11
  9.5 0.0 copy-start.10
  9.6 0.0 copy-start.9
  9.6 3.5 %second.1 = bf16[16,176,128]{2,1,0:T(8,128)(2,1)} custom-call(f32[1]{0:T(128)S(6)} %copy.18.depth_ref, f32[1,128]{1,0:T(1,128)S(1)} %get-tuple-element.22.energy_ref, bf16[648,1024]{1,0:T(8,128)(2,1)S(1)} %get-tuple-element.23.odd_ref, bf16[768,672]{1,0:T(8,128)(2,1)S(1)} %get-tuple-element.24.place_ref, bf16[672,648]{1,0:T(8,128)(2,1)S(1)} %get-tuple-element.25.wave_ref, ...), custom_call_target="tpu_custom_call" | custom-call | tf_op jit(solution)/shard_map/second/pallas_call | solution.py:545
  13.1 0.0 copy-start.2
  13.1 0.0 copy-start.1
  13.1 0.0 copy-start.3
  13.1 0.0 copy-start.4
  13.1 0.0 copy-start.5
  13.1 0.0 copy-start.7
  13.1 6.7 %all-to-all-start = ((bf16[16,176,128]{2,1,0:T(8,128)(2,1)}), bf16[16,176,128]{2,1,0:T(8,128)(2,1)S(1)}, u32[]{:S(2)}, u32[]{:S(2)}) async-start(bf16[16,176,128]{2,1,0:T(8,128)(2,1)} %second.1), calls=%async_computation | async-start | bytes 1441792 | tf_op jit(solution)/shard_map/all_to_all | solution.py:546
  19.8 0.0 copy-done.15
  19.8 1.2 %collective-permute-start = (bf16[2,216,128]{2,1,0:T(8,128)(2,1)S(1)}, bf16[2,216,128]{2,1,0:T(8,128)(2,1)S(1)}, u32[]{:S(2)}, u32[]{:S(2)}) collective-permute-start(bf16[2,216,128]{2,1,0:T(8,128)(2,1)S(1)} %copy-done.15), channel_id=1, source_target_pairs={{0,2},{1,3},{2,0},{3,1},{4,6},{5,7},{6,4},{7,5},{8,10},{9,11},{10,... | collective-permute-start | bytes 331784 | tf_op jit(solution)/shard_map/ppermute | solution.py:529
  21.1 0.0 copy-done.14
  21.1 1.2 %collective-permute-start.1 = (bf16[2,216,128]{2,1,0:T(8,128)(2,1)S(1)}, bf16[2,216,128]{2,1,0:T(8,128)(2,1)S(1)}, u32[]{:S(2)}, u32[]{:S(2)}) collective-permute-start(bf16[2,216,128]{2,1,0:T(8,128)(2,1)S(1)} %copy-done.14), channel_id=1, source_target_pairs={{0,4},{1,5},{2,6},{3,7},{4,8},{5,9},{6,10},{7,11},{8,12},{9,13},{1... | collective-permute-start | bytes 331784 | tf_op jit(solution)/shard_map/ppermute | solution.py:529
  22.3 0.0 copy-done.13
  22.3 1.2 %collective-permute-start.2 = (bf16[2,216,128]{2,1,0:T(8,128)(2,1)S(1)}, bf16[2,216,128]{2,1,0:T(8,128)(2,1)S(1)}, u32[]{:S(2)}, u32[]{:S(2)}) collective-permute-start(bf16[2,216,128]{2,1,0:T(8,128)(2,1)S(1)} %copy-done.13), channel_id=1, source_target_pairs={{0,6},{1,7},{2,4},{3,5},{4,10},{5,11},{6,8},{7,9},{8,14},{9,15},{1... | collective-permute-start | bytes 331784 | tf_op jit(solution)/shard_map/ppermute | solution.py:529
  23.5 0.0 copy-done.12
  23.5 1.2 %collective-permute-start.3 = (bf16[2,216,128]{2,1,0:T(8,128)(2,1)S(1)}, bf16[2,216,128]{2,1,0:T(8,128)(2,1)S(1)}, u32[]{:S(2)}, u32[]{:S(2)}) collective-permute-start(bf16[2,216,128]{2,1,0:T(8,128)(2,1)S(1)} %copy-done.12), channel_id=1, source_target_pairs={{0,8},{1,9},{2,10},{3,11},{4,12},{5,13},{6,14},{7,15},{8,0},{9,1},... | collective-permute-start | bytes 331784 | tf_op jit(solution)/shard_map/ppermute | solution.py:529
  24.6 0.0 copy-done.11
  24.6 2.1 %collective-permute-start.4 = (bf16[2,216,128]{2,1,0:T(8,128)(2,1)S(1)}, bf16[2,216,128]{2,1,0:T(8,128)(2,1)S(1)}, u32[]{:S(2)}, u32[]{:S(2)}) collective-permute-start(bf16[2,216,128]{2,1,0:T(8,128)(2,1)S(1)} %copy-done.11), channel_id=1, source_target_pairs={{0,10},{1,11},{2,8},{3,9},{4,14},{5,15},{6,12},{7,13},{8,2},{9,3},... | collective-permute-start | bytes 331784 | tf_op jit(solution)/shard_map/ppermute | solution.py:529
  26.7 0.9 %collective-permute-done.refs_1_ = bf16[2,216,128]{2,1,0:T(8,128)(2,1)S(1)} collective-permute-done((bf16[2,216,128]{2,1,0:T(8,128)(2,1)S(1)}, bf16[2,216,128]{2,1,0:T(8,128)(2,1)S(1)}, u32[]{:S(2)}, u32[]{:S(2)}) %collective-permute-start) | collective-permute-done | bytes 110624 | tf_op jit(solution)/shard_map/ppermute | solution.py:529
  27.7 0.0 copy-done.10
  27.7 1.5 %collective-permute-start.5 = (bf16[2,216,128]{2,1,0:T(8,128)(2,1)S(1)}, bf16[2,216,128]{2,1,0:T(8,128)(2,1)S(1)}, u32[]{:S(2)}, u32[]{:S(2)}) collective-permute-start(bf16[2,216,128]{2,1,0:T(8,128)(2,1)S(1)} %copy-done.10), channel_id=1, source_target_pairs={{0,12},{1,13},{2,14},{3,15},{4,0},{5,1},{6,2},{7,3},{8,4},{9,5},{1... | collective-permute-start | bytes 331784 | tf_op jit(solution)/shard_map/ppermute | solution.py:529
  29.1 18.2 %collective-permute-done.1.refs_2_ = bf16[2,216,128]{2,1,0:T(8,128)(2,1)S(1)} collective-permute-done((bf16[2,216,128]{2,1,0:T(8,128)(2,1)S(1)}, bf16[2,216,128]{2,1,0:T(8,128)(2,1)S(1)}, u32[]{:S(2)}, u32[]{:S(2)}) %collective-permute-start.1) | collective-permute-done | bytes 110624 | tf_op jit(solution)/shard_map/ppermute | solution.py:529
  47.3 0.0 copy-done.9
  47.3 0.0 collective-permute-start.6
  47.3 2.4 %collective-permute-done.2.refs_3_ = bf16[2,216,128]{2,1,0:T(8,128)(2,1)S(1)} collective-permute-done((bf16[2,216,128]{2,1,0:T(8,128)(2,1)S(1)}, bf16[2,216,128]{2,1,0:T(8,128)(2,1)S(1)}, u32[]{:S(2)}, u32[]{:S(2)}) %collective-permute-start.2) | collective-permute-done | bytes 110624 | tf_op jit(solution)/shard_map/ppermute | solution.py:529
  49.7 2.4 %collective-permute-done.3.refs_4_ = bf16[2,216,128]{2,1,0:T(8,128)(2,1)S(1)} collective-permute-done((bf16[2,216,128]{2,1,0:T(8,128)(2,1)S(1)}, bf16[2,216,128]{2,1,0:T(8,128)(2,1)S(1)}, u32[]{:S(2)}, u32[]{:S(2)}) %collective-permute-start.3) | collective-permute-done | bytes 110624 | tf_op jit(solution)/shard_map/ppermute | solution.py:529
  52.1 2.4 %collective-permute-done.4.refs_5_ = bf16[2,216,128]{2,1,0:T(8,128)(2,1)S(1)} collective-permute-done((bf16[2,216,128]{2,1,0:T(8,128)(2,1)S(1)}, bf16[2,216,128]{2,1,0:T(8,128)(2,1)S(1)}, u32[]{:S(2)}, u32[]{:S(2)}) %collective-permute-start.4) | collective-permute-done | bytes 110624 | tf_op jit(solution)/shard_map/ppermute | solution.py:529
  54.4 0.0 collective-permute-done.5.refs_6_
  54.4 2.8 %collective-permute-done.6.refs_7_ = bf16[2,216,128]{2,1,0:T(8,128)(2,1)S(1)} collective-permute-done((bf16[2,216,128]{2,1,0:T(8,128)(2,1)S(1)}, bf16[2,216,128]{2,1,0:T(8,128)(2,1)S(1)}, u32[]{:S(2)}, u32[]{:S(2)}) %collective-permute-start.6) | collective-permute-done | bytes 110624 | tf_op jit(solution)/shard_map/ppermute | solution.py:529
  57.3 0.0 copy-done.2
  57.3 0.0 copy-start.6
  57.3 1.0 %collective-permute-start.7 = (bf16[8,216,128]{2,1,0:T(8,128)(2,1)S(1)}, bf16[8,216,128]{2,1,0:T(8,128)(2,1)S(1)}, u32[]{:S(2)}, u32[]{:S(2)}) collective-permute-start(bf16[8,216,128]{2,1,0:T(8,128)(2,1)S(1)} %repack.1), channel_id=1, source_target_pairs={{0,1},{1,0},{2,3},{3,2},{4,5},{5,4},{6,7},{7,6},{8,9},{9,8},{10,11... | collective-permute-start | bytes 1327112 | tf_op jit(solution)/shard_map/ppermute | solution.py:557
  58.4 1.4 %collective-permute-done.7.refs_8_ = bf16[8,216,128]{2,1,0:T(8,128)(2,1)S(1)} collective-permute-done((bf16[8,216,128]{2,1,0:T(8,128)(2,1)S(1)}, bf16[8,216,128]{2,1,0:T(8,128)(2,1)S(1)}, u32[]{:S(2)}, u32[]{:S(2)}) %collective-permute-start.7) | collective-permute-done | bytes 442400 | tf_op jit(solution)/shard_map/ppermute | solution.py:557
  59.8 0.0 copy-done.1
  59.8 0.0 copy-done.3
  59.8 0.0 copy-done.4
  59.8 0.0 copy-done.5
  59.8 0.0 copy-done.7
  59.8 4.2 %even.1 = (f32[672,1024]{1,0:T(8,128)S(1)}, bf16[512,256]{1,0:T(8,128)(2,1)S(1)}, bf16[672,128]{1,0:T(8,128)(2,1)S(1)}) custom-call(s32[16]{0:T(128)S(1)} %copy-done.7, bf16[512,256]{1,0:T(8,128)(2,1)S(1)} %copy-done.4, bf16[128,256]{1,0:T(8,128)(2,1)S(1)} %copy-done.3, f32[32,640]{1,0:T(8,128)S(1)} %copy-done.5, bf16[640,1024]{1,0:T(8,128)(2,1)S(1)} %copy-done.1, ...), custom_call_target="tpu_custom_call" | custom-call | tf_op jit(solution)/shard_map/even/pallas_call | solution.py:563
  64.0 0.0 copy-start
  64.1 1.5 %copy-done = f32[672,1024]{1,0:T(8,128)} copy-done((f32[672,1024]{1,0:T(8,128)}, f32[672,1024]{1,0:T(8,128)S(1)}, u32[]{:S(2)}) %copy-start) | copy-done | bytes 2752536
  65.6 0.0 all-to-all-done.arrived_hbm
  65.6 0.0 copy-start.8
  65.6 0.9 %copy-done.8 = bf16[16,176,128]{2,1,0:T(8,128)(2,1)} copy-done((bf16[16,176,128]{2,1,0:T(8,128)(2,1)}, bf16[16,176,128]{2,1,0:T(8,128)(2,1)S(1)}, u32[]{:S(2)}) %copy-start.8) | copy-done | bytes 720920
  66.4 0.0 copy-done.6
  66.4 5.2 %last.1 = f32[672,2048]{1,0:T(8,128)} custom-call(bf16[16,176,128]{2,1,0:T(8,128)(2,1)} %copy-done.8, bf16[512,256]{1,0:T(8,128)(2,1)S(1)} %get-tuple-element.36.forward_hbm, bf16[128,256]{1,0:T(8,128)(2,1)S(1)} %copy-done.3, f32[32,512]{1,0:T(8,128)S(1)} %copy-done.6, bf16[672,128]{1,0:T(8,128)(2,1)S(1)} %get-tuple-element.37.mixed_hbm, ...), custom_call_target="tpu_custom_call" | custom-call | tf_op jit(solution)/shard_map/last/pallas_call | solution.py:586
  (1 shorter events, 0.0 us)
Async XLA Ops:
  9.5 10.3 %copy-start.15 = (bf16[2,216,128]{2,1,0:T(8,128)(2,1)S(1)}, bf16[2,216,128]{2,1,0:T(8,128)(2,1)}, u32[]{:S(2)}) copy-start(bf16[2,216,128]{2,1,0:T(8,128)(2,1)} %get-tuple-element.29) | copy-start | bytes 331780
  9.5 11.6 %copy-start.14 = (bf16[2,216,128]{2,1,0:T(8,128)(2,1)S(1)}, bf16[2,216,128]{2,1,0:T(8,128)(2,1)}, u32[]{:S(2)}) copy-start(bf16[2,216,128]{2,1,0:T(8,128)(2,1)} %get-tuple-element.30) | copy-start | bytes 331780
  9.5 12.8 %copy-start.13 = (bf16[2,216,128]{2,1,0:T(8,128)(2,1)S(1)}, bf16[2,216,128]{2,1,0:T(8,128)(2,1)}, u32[]{:S(2)}) copy-start(bf16[2,216,128]{2,1,0:T(8,128)(2,1)} %get-tuple-element.31) | copy-start | bytes 331780
  9.5 13.9 %copy-start.12 = (bf16[2,216,128]{2,1,0:T(8,128)(2,1)S(1)}, bf16[2,216,128]{2,1,0:T(8,128)(2,1)}, u32[]{:S(2)}) copy-start(bf16[2,216,128]{2,1,0:T(8,128)(2,1)} %get-tuple-element.32) | copy-start | bytes 331780
  9.5 15.1 %copy-start.11 = (bf16[2,216,128]{2,1,0:T(8,128)(2,1)S(1)}, bf16[2,216,128]{2,1,0:T(8,128)(2,1)}, u32[]{:S(2)}) copy-start(bf16[2,216,128]{2,1,0:T(8,128)(2,1)} %get-tuple-element.33) | copy-start | bytes 331780
  9.5 18.1 %copy-start.10 = (bf16[2,216,128]{2,1,0:T(8,128)(2,1)S(1)}, bf16[2,216,128]{2,1,0:T(8,128)(2,1)}, u32[]{:S(2)}) copy-start(bf16[2,216,128]{2,1,0:T(8,128)(2,1)} %get-tuple-element.34) | copy-start | bytes 331780
  9.6 37.8 %copy-start.9 = (bf16[2,216,128]{2,1,0:T(8,128)(2,1)S(1)}, bf16[2,216,128]{2,1,0:T(8,128)(2,1)}, u32[]{:S(2)}) copy-start(bf16[2,216,128]{2,1,0:T(8,128)(2,1)} %get-tuple-element.35) | copy-start | bytes 331780
  13.1 44.2 %copy-start.2 = (bf16[2,216,128]{2,1,0:T(8,128)(2,1)S(1)}, bf16[2,216,128]{2,1,0:T(8,128)(2,1)}, u32[]{:S(2)}) copy-start(bf16[2,216,128]{2,1,0:T(8,128)(2,1)} %get-tuple-element.28.refs_0_) | copy-start | bytes 331780
  13.1 46.7 %copy-start.1 = (bf16[640,1024]{1,0:T(8,128)(2,1)S(1)}, bf16[640,1024]{1,0:T(8,128)(2,1)}, u32[]{:S(2)}) copy-start(bf16[640,1024]{1,0:T(8,128)(2,1)} %constant.33.clone.table_hbm) | copy-start | bytes 3932164
  13.1 46.7 %copy-start.3 = (bf16[128,256]{1,0:T(8,128)(2,1)S(1)}, bf16[128,256]{1,0:T(8,128)(2,1)}, u32[]{:S(2)}) copy-start(bf16[128,256]{1,0:T(8,128)(2,1)} %constant.31.clone.inverse_hbm) | copy-start | bytes 196612
  13.1 46.7 %copy-start.4 = (bf16[512,256]{1,0:T(8,128)(2,1)S(1)}, bf16[512,256]{1,0:T(8,128)(2,1)}, u32[]{:S(2)}) copy-start(bf16[512,256]{1,0:T(8,128)(2,1)} %constant.30.clone.forward_hbm) | copy-start | bytes 786436
  13.1 46.7 %copy-start.5 = (f32[32,640]{1,0:T(8,128)S(1)}, f32[32,640]{1,0:T(8,128)}, u32[]{:S(2)}) copy-start(f32[32,640]{1,0:T(8,128)} %constant.32.clone.response_hbm) | copy-start | bytes 245764
  13.1 46.7 %copy-start.7 = (s32[16]{0:T(128)S(1)}, s32[16]{0:T(128)}, u32[]{:S(2)}) copy-start(s32[16]{0:T(128)} %slot_ref.1) | copy-start | bytes 196
  13.1 52.4 %all-to-all-start = ((bf16[16,176,128]{2,1,0:T(8,128)(2,1)}), bf16[16,176,128]{2,1,0:T(8,128)(2,1)S(1)}, u32[]{:S(2)}, u32[]{:S(2)}) async-start(bf16[16,176,128]{2,1,0:T(8,128)(2,1)} %second.1), calls=%async_computation | async-start | bytes 1441792 | tf_op jit(solution)/shard_map/all_to_all | solution.py:546
  19.8 7.8 %collective-permute-start = (bf16[2,216,128]{2,1,0:T(8,128)(2,1)S(1)}, bf16[2,216,128]{2,1,0:T(8,128)(2,1)S(1)}, u32[]{:S(2)}, u32[]{:S(2)}) collective-permute-start(bf16[2,216,128]{2,1,0:T(8,128)(2,1)S(1)} %copy-done.15), channel_id=1, source_target_pairs={{0,2},{1,3},{2,0},{3,1},{4,6},{5,7},{6,4},{7,5},{8,10},{9,11},{10,... | collective-permute-start | bytes 331784 | tf_op jit(solution)/shard_map/ppermute | solution.py:529
  21.1 26.3 %collective-permute-start.1 = (bf16[2,216,128]{2,1,0:T(8,128)(2,1)S(1)}, bf16[2,216,128]{2,1,0:T(8,128)(2,1)S(1)}, u32[]{:S(2)}, u32[]{:S(2)}) collective-permute-start(bf16[2,216,128]{2,1,0:T(8,128)(2,1)S(1)} %copy-done.14), channel_id=1, source_target_pairs={{0,4},{1,5},{2,6},{3,7},{4,8},{5,9},{6,10},{7,11},{8,12},{9,13},{1... | collective-permute-start | bytes 331784 | tf_op jit(solution)/shard_map/ppermute | solution.py:529
  22.3 27.4 %collective-permute-start.2 = (bf16[2,216,128]{2,1,0:T(8,128)(2,1)S(1)}, bf16[2,216,128]{2,1,0:T(8,128)(2,1)S(1)}, u32[]{:S(2)}, u32[]{:S(2)}) collective-permute-start(bf16[2,216,128]{2,1,0:T(8,128)(2,1)S(1)} %copy-done.13), channel_id=1, source_target_pairs={{0,6},{1,7},{2,4},{3,5},{4,10},{5,11},{6,8},{7,9},{8,14},{9,15},{1... | collective-permute-start | bytes 331784 | tf_op jit(solution)/shard_map/ppermute | solution.py:529
  23.5 28.6 %collective-permute-start.3 = (bf16[2,216,128]{2,1,0:T(8,128)(2,1)S(1)}, bf16[2,216,128]{2,1,0:T(8,128)(2,1)S(1)}, u32[]{:S(2)}, u32[]{:S(2)}) collective-permute-start(bf16[2,216,128]{2,1,0:T(8,128)(2,1)S(1)} %copy-done.12), channel_id=1, source_target_pairs={{0,8},{1,9},{2,10},{3,11},{4,12},{5,13},{6,14},{7,15},{8,0},{9,1},... | collective-permute-start | bytes 331784 | tf_op jit(solution)/shard_map/ppermute | solution.py:529
  24.6 29.8 %collective-permute-start.4 = (bf16[2,216,128]{2,1,0:T(8,128)(2,1)S(1)}, bf16[2,216,128]{2,1,0:T(8,128)(2,1)S(1)}, u32[]{:S(2)}, u32[]{:S(2)}) collective-permute-start(bf16[2,216,128]{2,1,0:T(8,128)(2,1)S(1)} %copy-done.11), channel_id=1, source_target_pairs={{0,10},{1,11},{2,8},{3,9},{4,14},{5,15},{6,12},{7,13},{8,2},{9,3},... | collective-permute-start | bytes 331784 | tf_op jit(solution)/shard_map/ppermute | solution.py:529
  27.7 26.8 %collective-permute-start.5 = (bf16[2,216,128]{2,1,0:T(8,128)(2,1)S(1)}, bf16[2,216,128]{2,1,0:T(8,128)(2,1)S(1)}, u32[]{:S(2)}, u32[]{:S(2)}) collective-permute-start(bf16[2,216,128]{2,1,0:T(8,128)(2,1)S(1)} %copy-done.10), channel_id=1, source_target_pairs={{0,12},{1,13},{2,14},{3,15},{4,0},{5,1},{6,2},{7,3},{8,4},{9,5},{1... | collective-permute-start | bytes 331784 | tf_op jit(solution)/shard_map/ppermute | solution.py:529
  47.3 9.9 %collective-permute-start.6 = (bf16[2,216,128]{2,1,0:T(8,128)(2,1)S(1)}, bf16[2,216,128]{2,1,0:T(8,128)(2,1)S(1)}, u32[]{:S(2)}, u32[]{:S(2)}) collective-permute-start(bf16[2,216,128]{2,1,0:T(8,128)(2,1)S(1)} %copy-done.9), channel_id=1, source_target_pairs={{0,14},{1,15},{2,12},{3,13},{4,2},{5,3},{6,0},{7,1},{8,6},{9,7},{1... | collective-permute-start | bytes 331784 | tf_op jit(solution)/shard_map/ppermute | solution.py:529
  57.3 9.1 %copy-start.6 = (f32[32,512]{1,0:T(8,128)S(1)}, f32[32,512]{1,0:T(8,128)}, u32[]{:S(2)}) copy-start(f32[32,512]{1,0:T(8,128)} %constant.34.clone.response_hbm) | copy-start | bytes 196612
  57.3 2.5 %collective-permute-start.7 = (bf16[8,216,128]{2,1,0:T(8,128)(2,1)S(1)}, bf16[8,216,128]{2,1,0:T(8,128)(2,1)S(1)}, u32[]{:S(2)}, u32[]{:S(2)}) collective-permute-start(bf16[8,216,128]{2,1,0:T(8,128)(2,1)S(1)} %repack.1), channel_id=1, source_target_pairs={{0,1},{1,0},{2,3},{3,2},{4,5},{5,4},{6,7},{7,6},{8,9},{9,8},{10,11... | collective-permute-start | bytes 1327112 | tf_op jit(solution)/shard_map/ppermute | solution.py:557
  64.0 1.5 %copy-start = (f32[672,1024]{1,0:T(8,128)}, f32[672,1024]{1,0:T(8,128)S(1)}, u32[]{:S(2)}) copy-start(f32[672,1024]{1,0:T(8,128)S(1)} %get-tuple-element.38.even_hbm) | copy-start | bytes 8257540
  65.6 0.9 %copy-start.8 = (bf16[16,176,128]{2,1,0:T(8,128)(2,1)}, bf16[16,176,128]{2,1,0:T(8,128)(2,1)S(1)}, u32[]{:S(2)}) copy-start(bf16[16,176,128]{2,1,0:T(8,128)(2,1)S(1)} %all-to-all-done.arrived_hbm) | copy-start | bytes 2162692

commit v2 on v1

--- a/solution.py
+++ b/solution.py
@@ -27,7 +27,6 @@
 LANES = 128
 HALF = 64
 UNIT = 8
-STRIP = 512
 ALL_VMEM = 60 << 20
 MOST_VMEM = 53 << 20
 FRONT_VMEM = 52 << 20
@@ -39,15 +38,28 @@
 
 
 def bin_tiles():
-    even = np.arange(0, FREQ, 2)
     odd = np.arange(1, FREQ, 2)
-    whole = len(even) // HALF
-    left = len(even) - whole * HALF
-    assert 2 * left == HALF and len(odd) == len(even)
-    even_tiles = [even[j * HALF : (j + 1) * HALF] for j in range(whole)]
+    fours = np.arange(0, FREQ, 4)
+    twos = np.arange(2, FREQ, 4)
+    whole = len(odd) // HALF
+    left = len(odd) - whole * HALF
+    half = len(fours) // HALF
+    assert 2 * left == HALF and 2 * half == whole and len(fours) == len(twos)
     odd_tiles = [odd[left + j * HALF : left + (j + 1) * HALF] for j in range(whole)]
-    mixed = np.concatenate([even[whole * HALF :], odd[:left]])
+    even_tiles = [b[j * HALF : (j + 1) * HALF] for b in (fours, twos) for j in range(half)]
+    mixed = np.concatenate([fours[half * HALF :], twos[half * HALF :], odd[:left]])
     return even_tiles, odd_tiles, mixed
+
+
+def quarter_table(n_samples, tiles, mixed):
+    full = time_table(n_samples, tiles + [mixed], 0)[: n_samples // 4].astype(np.float32)
+    columns = len(tiles) * LANES
+    parts = []
+    for h in range(2):
+        keep = np.tile(mixed % 4 == 2 * h, 2)[None, :]
+        mine = full[:, h * columns // 2 : (h + 1) * columns // 2]
+        parts.append(np.concatenate([mine, np.where(keep, full[:, columns:], 0.0)], axis=1).T)
+    return to_bf16(np.stack(parts))
 
 
 def time_table(n_samples, tiles, parity):
@@ -194,15 +206,13 @@
 
 
 class Layout:
-    def __init__(self, per, tiles, spare):
+    def __init__(self, per, tiles):
+        assert per >= 3
         self.whole = per // UNIT
         self.left = per % UNIT
         self.tiles = tiles
         self.shared = UNIT // self.left if self.left else 1
-        rows = tiles * self.left
         self.left_units = -(-tiles // self.shared) if self.left else 0
-        if spare and rows - (self.left_units - 1) * self.shared * self.left == UNIT or spare and not self.left_units:
-            self.left_units += 1
         self.units = self.whole * tiles + self.left_units
 
     def unit(self, tile, u):
@@ -225,6 +235,9 @@
 
 def place_message(placed, layout, frame, store, i, energy=None):
     mine = placed[i * frame : (i + 1) * frame]
+    if energy is not None:
+        top = jnp.concatenate([with_energy(mine[:UNIT, :LANES], energy), mine[:UNIT, LANES:]], axis=1)
+        mine = top if frame == UNIT else jnp.concatenate([top, mine[UNIT:]], axis=0)
     parts = [mine[: layout.whole * UNIT, t * LANES : (t + 1) * LANES] for t in range(layout.tiles)] if layout.whole else []
     left = [jnp.zeros((UNIT, LANES), F32) for _ in range(layout.left_units)]
     if layout.left:
@@ -234,9 +247,6 @@
             shift = t % layout.shared * layout.left
             unit = jnp.where(row < layout.left, unit, 0.0)
             left[t // layout.shared] += pltpu.roll(unit, shift, 0) if shift else unit
-    if energy is not None:
-        row = lax.broadcasted_iota(jnp.int32, (UNIT, LANES), 0)
-        left[-1] = jnp.where(row == UNIT - 1, energy, left[-1])
     store(jnp.concatenate(parts + left, axis=0).astype(BF))
 
 
@@ -244,9 +254,14 @@
     total = jnp.sum(energy, axis=1, keepdims=True)
     high = total.astype(BF).astype(F32)
     middle = (total - high).astype(BF).astype(F32)
-    low = total - high - middle
-    lane = lax.broadcasted_iota(jnp.int32, (1, LANES), 1)
-    return jnp.where(lane == 0, high, jnp.where(lane == 1, middle, jnp.where(lane == 2, low, 0.0)))
+    return high, middle, total - high - middle
+
+
+def with_energy(unit, pieces):
+    row = lax.broadcasted_iota(jnp.int32, (UNIT, LANES), 0)
+    lane = lax.broadcasted_iota(jnp.int32, (UNIT, LANES), 1)
+    value = jnp.where(row == 0, pieces[0], jnp.where(row == 1, pieces[1], jnp.where(row == 2, pieces[2], 0.0)))
+    return jnp.where(lane == HALF, value, unit)
 
 
 def into(ref, index=None):
@@ -269,16 +284,16 @@
 def front_kernel(per, frame, layout, records, count):
     def kernel(depth_ref, receiver_ref, home_ref, vertical_hbm, wave_hbm, traces_hbm, table_hbm, mixed_hbm, *refs):
         later_hbm = refs[:2]
-        *messages, odd_ref, place_ref, wave_ref, energy_ref = refs[2 : 6 + count]
+        *messages, sum_ref, place_ref, wave_ref, energy_ref = refs[2 : 6 + count]
         later = refs[6 + count : 8 + count]
-        vertical_ref, traces_ref, table_ref, mixed_ref, sum_ref, placed_ref, factors_ref, sems = refs[8 + count :]
+        vertical_ref, traces_ref, table_ref, mixed_ref, odd_ref, placed_ref, factors_ref, sems = refs[8 + count :]
         me = lax.axis_index("shard")
         n_channels, n_samples = traces_ref.shape
         half = n_samples // 2
         steps = 3
         step = n_channels // steps
         pairs = [(traces_hbm.at[pl.ds(s * step, step), :], traces_ref.at[pl.ds(s * step, step), :]) for s in range(steps)]
-        pairs = [(vertical_hbm, vertical_ref), (wave_hbm, wave_ref), *pairs, (table_hbm, table_ref), (mixed_hbm, mixed_ref)]
+        pairs = [(wave_hbm, wave_ref), *pairs, (table_hbm, table_ref), (mixed_hbm, mixed_ref), (vertical_hbm, vertical_ref)]
         copies = start_all(pairs, sems)
         n_rec = home_ref.shape[0]
         home = home_ref[...].reshape(1, n_rec)
@@ -294,24 +309,23 @@
         picked = lax.broadcasted_iota(jnp.int32, (records * frame, n_channels), 0) == target
         picked = jnp.where(picked, 1.0, 0.0).astype(BF)
         copies[0].wait()
-        copies[1].wait()
         place_ref[...] = lax.dot_general(picked, wave_ref[...], (((1,), (1,)), ((), ())), preferred_element_type=F32).astype(BF)
         outs = start_all(list(zip(later_hbm, later)), sems, len(copies))
         for s in range(steps):
-            copies[2 + s].wait()
+            copies[1 + s].wait()
             part = pl.ds(s * step, step)
             first = traces_ref[part, :half]
             second = traces_ref[part, half:]
             sum_ref[part, :] = (first + second).astype(BF)
             odd_ref[part, :] = (first - second).astype(BF)
-        for c in copies[-2:]:
+        for c in copies[-3:]:
             c.wait()
         spec = []
         for t in range(0, layout.tiles, 2):
             cols = slice(t * LANES, min(t + 2, layout.tiles) * LANES)
-            got = dot(sum_ref[...], table_ref[:, cols])
+            got = dot(odd_ref[...], table_ref[:, cols])
             if t + 2 > layout.tiles:
-                got = got + dot(odd_ref[...], mixed_ref[...])
+                got = got + dot(sum_ref[...], mixed_ref[...])
             spec.append(got.astype(BF))
             store_factors(factors_ref, vertical_ref, depth_ref[0], n_channels, t)
         spec = jnp.concatenate(spec, axis=1)
@@ -327,10 +341,10 @@
 
 
 def second_kernel(frame, layout, records):
-    def kernel(depth_ref, energy_ref, odd_ref, place_ref, wave_ref, table_ref, vertical_ref, message_ref, placed_ref, factors_ref):
+    def kernel(depth_ref, energy_ref, sum_ref, place_ref, wave_ref, table_ref, vertical_ref, message_ref, placed_ref, factors_ref):
         me = lax.axis_index("shard")
-        store_factors(factors_ref, vertical_ref, depth_ref[0], odd_ref.shape[0])
-        spec = dot(odd_ref[...], table_ref[...]).astype(BF)
+        store_factors(factors_ref, vertical_ref, depth_ref[0], sum_ref.shape[0])
+        spec = dot(sum_ref[...], table_ref[...]).astype(BF)
         placed_ref[...] = dot(place_ref[...], lift(spec, factors_ref, 0, wave_ref))
         pieces = split_energy(energy_ref[...] + energy_of(placed_ref[...]))
         for i in range(records):
@@ -384,7 +398,7 @@
     return kernel
 
 
-def even_kernel(per, block, layout, records, n_sources):
+def odd_kernel(per, block, layout, records, n_sources):
     def kernel(slot_ref, forward_hbm, inverse_hbm, response_hbm, table_hbm, *refs):
         sources = refs[:n_sources]
         (out_hbm, forward_b_hbm, mixed_hbm, out_ref, forward_b_ref, forward_ref, plain_ref, inverse_ref, response_ref, table_ref,
@@ -421,24 +435,24 @@
 
 
 def last_kernel(per, block, layout, n_traces, records):
-    def kernel(arrived_hbm, forward_hbm, inverse_hbm, response_hbm, mixed_hbm, odd_table_hbm, even_hbm,
-               out_hbm, arrived_ref, forward_ref, inverse_ref, response_ref, odd_table_ref, even_ref, filtered_ref, out_ref, sems):
-        half = even_ref.shape[1]
-        strip = STRIP
+    def kernel(arrived_hbm, forward_hbm, inverse_hbm, response_hbm, mixed_hbm, table_hbm, odd_hbm,
+               out_hbm, arrived_ref, forward_ref, inverse_ref, response_ref, table_ref, odd_ref, filtered_ref, out_ref, sems):
+        quarter = odd_ref.shape[1] // 2
         cuts = [pl.ds(g * records, min(block, per - g) * records) for g in range(0, per, block)]
         mixed = filtered_ref.at[:, pl.ds(layout.tiles * LANES, LANES)]
         first = [(arrived_hbm, arrived_ref), (forward_hbm, forward_ref), (inverse_hbm, inverse_ref), (response_hbm, response_ref)]
-        fetch = start_all(first + [(odd_table_hbm, odd_table_ref), (mixed_hbm, mixed)], sems)
-        fetch += start_all([(even_hbm.at[c, :], even_ref.at[c, :]) for c in cuts], sems, len(fetch))
+        fetch = start_all(first + [(table_hbm, table_ref), (mixed_hbm, mixed)], sems)
+        fetch += start_all([(odd_hbm.at[c, :], odd_ref.at[c, :]) for c in cuts], sems, len(fetch))
         for c in fetch[:4]:
             c.wait()
         arrived = [arrived_ref[s] for s in range(records)]
         row = lax.broadcasted_iota(jnp.int32, (UNIT, LANES), 0)
         lane = lax.broadcasted_iota(jnp.int32, (UNIT, LANES), 1)
-        ends = sum(a[(layout.units - 1) * UNIT :].astype(F32) for a in arrived)
-        ends = jnp.where((row == UNIT - 1) & (lane < 3), ends, 0.0)
-        energy = jnp.sum(ends, keepdims=True)
+        at = layout.unit(0, 0)[0] * UNIT
+        ends = sum(a[at : at + UNIT].astype(F32) for a in arrived)
+        energy = jnp.sum(jnp.where((row < 3) & (lane == HALF), ends, 0.0), keepdims=True)
         scale = lax.rsqrt(2.0 * FREQ * (energy * (1.0 / (n_traces * FREQ)) + energy_eps))
+        whole = layout.tiles * LANES
         copies = []
         for b in range(len(cuts)):
             filter_gathers(arrived, layout, forward_ref, inverse_ref, response_ref, filtered_ref, per, block, (b,))
@@ -447,16 +461,15 @@
                     c.wait()
             fetch[6 + b].wait()
             here = cuts[b]
-            for s in range(0, half, strip):
-                cols = slice(s, s + strip)
-                odd = dot(filtered_ref[here, :], odd_table_ref[:, cols])
-                even = even_ref[here, cols]
-                out_ref[here, cols] = (even + odd) * scale
-                out_ref[here, half + s : half + s + strip] = (even - odd) * scale
-                pairs = []
-                for there in (pl.ds(s, strip), pl.ds(half + s, strip)):
-                    pairs.append((out_ref.at[here, there], out_hbm.at[here, there]))
-                copies += start_all(pairs, sems, len(fetch) + len(copies))
+            left = filtered_ref[here, whole:]
+            fours = dot(jnp.concatenate([filtered_ref[here, : whole // 2], left], axis=1), table_ref[0])
+            twos = dot(jnp.concatenate([filtered_ref[here, whole // 2 : whole], left], axis=1), table_ref[1])
+            for q, even in enumerate((fours + twos, fours - twos)):
+                odd = odd_ref[here, q * quarter : (q + 1) * quarter]
+                for p, value in enumerate((even + odd, even - odd)):
+                    there = pl.ds((2 * p + q) * quarter, quarter)
+                    out_ref[here, there] = value * scale
+                    copies += start_all([(out_ref.at[here, there], out_hbm.at[here, there])], sems, len(fetch) + len(copies))
         for c in copies:
             c.wait()
 
@@ -473,16 +486,16 @@
     frame = -(-per // UNIT) * UNIT
     even_tiles, odd_tiles, mixed = bin_tiles()
     n_whole = len(even_tiles)
-    layout = Layout(per, n_whole + 1, False)
-    layout_b = Layout(per, n_whole, True)
+    layout = Layout(per, n_whole + 1)
+    layout_b = Layout(per, n_whole)
     wave = wave_table(n_channels)
-    even_table = time_table(n_samples, even_tiles + [mixed], 0)
     odd_table = time_table(n_samples, odd_tiles + [mixed], 1)
-    mixed_odd = np.ascontiguousarray(odd_table[:, n_whole * LANES :])
-    odd_whole = np.ascontiguousarray(odd_table[:, : n_whole * LANES])
+    even_whole = time_table(n_samples, even_tiles, 0)
+    mixed_even = time_table(n_samples, [mixed], 0)
+    back_table = quarter_table(n_samples, even_tiles, mixed)
     pad_bins = np.zeros((HALF,), np.int64)
-    vertical = vertical_table(n_channels, n_samples, even_tiles + [mixed, pad_bins])
-    vertical_b = vertical_table(n_channels, n_samples, odd_tiles)
+    vertical = vertical_table(n_channels, n_samples, odd_tiles + [mixed, pad_bins])
+    vertical_b = vertical_table(n_channels, n_samples, even_tiles)
     pairwise = records <= 16
 
     smem = pl.BlockSpec(memory_space=pltpu.SMEM)
@@ -497,15 +510,16 @@
 
     n = records // 4
     planes = records // 2 if pairwise else 1
-    *sources, odd, place, wave_kept, energy, odd_kept, vertical_kept = pl.pallas_call(
+    made = pltpu.VMEM if pairwise else jax.ShapeDtypeStruct
+    *sources, sums, place, wave_kept, energy, even_kept, vertical_kept = pl.pallas_call(
         front_kernel(per, frame, layout, records, planes),
         out_shape=(
-            *(jax.ShapeDtypeStruct((records // planes, layout.units * UNIT, LANES), BF) for _ in range(planes)),
+            *(made((records // planes, layout.units * UNIT, LANES), BF) for _ in range(planes)),
             pltpu.VMEM((n_channels, half), BF),
             pltpu.VMEM((records * frame, wave.shape[0]), BF),
             scratch(wave),
             pltpu.VMEM((1, LANES), F32),
-            scratch(odd_whole),
+            scratch(even_whole),
             scratch(vertical_b),
         ),
         in_specs=[smem, vmem, vmem] + [hbm] * 7,
@@ -513,8 +527,8 @@
         scratch_shapes=[
             scratch(vertical),
             scratch(traces),
-            scratch(even_table),
-            scratch(mixed_odd),
+            scratch(odd_table),
+            scratch(mixed_even),
             pltpu.VMEM((n_channels, half), BF),
             pltpu.VMEM((records * frame, (n_whole + 1) * LANES), F32),
             pltpu.VMEM((2, n_whole + 1, wave.shape[0] // 2, LANES), F32),
@@ -522,7 +536,7 @@
         ],
         compiler_params=pltpu.CompilerParams(vmem_limit_bytes=FRONT_VMEM),
         name="front",
-    )(cable_depth, receiver, gather_home, vertical, wave, traces, even_table, mixed_odd, odd_whole, vertical_b)
+    )(cable_depth, receiver, gather_home, vertical, wave, traces, odd_table, mixed_even, even_whole, vertical_b)
     if pairwise:
         for chip in chips(records):
             route = [(s, partner(s, chip // 2, chip % 2 * 2, n, 1)) for s in range(records)]
@@ -542,7 +556,7 @@
         compiler_params=shared,
         name="second",
     )
-    message_b = second(cable_depth, energy, odd, place, wave_kept, odd_kept, vertical_kept)
+    message_b = second(cable_depth, energy, sums, place, wave_kept, even_kept, vertical_kept)
     arrived_b = lax.all_to_all(message_b, "shard", split_axis=0, concat_axis=0, tiled=True)
 
     if pairwise:
@@ -558,10 +572,10 @@
 
     forward = shot_forward(records, block)
     inverse = shot_inverse(records)
-    response = response_table(records, n_samples, even_tiles + [mixed])
-    even_inverse = np.ascontiguousarray(even_table.T)
-    even, forward_b, mixed_part = pl.pallas_call(
-        even_kernel(per, block, layout, records, len(sources)),
+    response = response_table(records, n_samples, odd_tiles + [mixed])
+    odd_inverse = np.ascontiguousarray(odd_table.T)
+    odd, forward_b, mixed_part = pl.pallas_call(
+        odd_kernel(per, block, layout, records, len(sources)),
         out_shape=(
             jax.ShapeDtypeStruct((per * records, half), F32),
             jax.ShapeDtypeStruct(forward.shape, BF),
@@ -576,13 +590,13 @@
             scratch(forward),
             scratch(inverse),
             scratch(response),
-            scratch(even_inverse),
+            scratch(odd_inverse),
             pltpu.VMEM((per * records, (n_whole + 1) * LANES), BF),
             pltpu.SemaphoreType.DMA((7,)),
         ],
         compiler_params=shared,
-        name="even",
-    )(shot_slot, forward, inverse, response, even_inverse, *sources)
+        name="odd",
+    )(shot_slot, forward, inverse, response, odd_inverse, *sources)
     out = pl.pallas_call(
         last_kernel(per, block, layout_b, n_channels * records, records),
         out_shape=jax.ShapeDtypeStruct((per * records, n_samples), F32),
@@ -593,15 +607,15 @@
             scratch(forward),
             scratch(inverse),
             pltpu.VMEM((2 * records, n_whole * LANES), F32),
-            scratch(odd_table.T),
+            scratch(back_table),
             pltpu.VMEM((per * records, half), F32),
             pltpu.VMEM((per * records, (n_whole + 1) * LANES), BF),
             pltpu.VMEM((per * records, n_samples), F32),
-            pltpu.SemaphoreType.DMA((6 + -(-per // block) * (1 + 2 * (half // STRIP)),)),
+            pltpu.SemaphoreType.DMA((6 + 5 * -(-per // block),)),
         ],
         compiler_params=most,
         name="last",
-    )(arrived_b, forward_b, inverse, response_table(records, n_samples, odd_tiles), mixed_part, np.ascontiguousarray(odd_table.T), even)
+    )(arrived_b, forward_b, inverse, response_table(records, n_samples, even_tiles), mixed_part, back_table, odd)
     return out.reshape(per, records, n_samples)
 
 

time: 72 us -> 70.4 us (0.978)
  Pallas kernels: 21.8 us -> 20.9 us
    pallas_call x1, Pallas kernels: 8.83 us -> 7.9 us  [shards(): pl.pallas_call(front_kernel(per, frame, layout, records, planes), out_sha...]
    unnamed x32 -> x16, local copies, waits for them, and re-layouts: 2.45 us -> 2.42 us
where the time goes in v2:
time: 70.4 us; the launch traced here: 70.2 us
  waiting for transfers between devices  30 us (43%)
  Pallas kernels  20.9 us (30%)
  starting transfers between devices  15.9 us (23%)
  local copies, waits for them, and re-layouts  2.42 us (3%)
  between operations  0.89 us (1%)
    ppermute x7, waiting for transfers between devices, shards(): sources[chip] = lax.ppermute(sources[chip], 'shard', route)  28.5 us
    ppermute x7, starting transfers between devices, shards(): sources[chip] = lax.ppermute(sources[chip], 'shard', route)  8.2 us
    pallas_call x1, Pallas kernels, shards(): pl.pallas_call(front_kernel(per, frame, layout, records, planes), out_sha...  7.9 us
    all_to_all x1, starting transfers between devices, shards(): lax.all_to_all(message_b, 'shard', split_axis=0, concat_axis=0, tiled=True)  6.7 us
    pallas_call x1, Pallas kernels, shards(): pl.pallas_call(last_kernel(per, block, layout_b, n_channels * records, re...  5.25 us
    pallas_call x1, Pallas kernels, shards(): pl.pallas_call(odd_kernel(per, block, layout, records, len(sources)), out...  4.23 us
    pallas_call x1, Pallas kernels, shards(): second(cable_depth, energy, sums, place, wave_kept, even_kept, vertical_k...  3.54 us
    unnamed x16, local copies, waits for them, and re-layouts  2.42 us
  transfers between devices with their start and end apart: 9, of which 7 were waited for; matrix products, arithmetic and copies ran while one was open for 0% of the time, Pallas kernels for 6%

profile of v2, /device:TPU:9, one launch (start us, length us, event | category | flops | bytes accessed | tf_op | source)
XLA Modules:
  0.0 70.2 jit_solution(10533743463074846581)
XLA Ops:
  0.7 7.9 %front.1 = (bf16[2,216,128]{2,1,0:T(8,128)(2,1)S(1)}, bf16[2,216,128]{2,1,0:T(8,128)(2,1)S(1)}, bf16[2,216,128]{2,1,0:T(8,128)(2,1)S(1)}, bf16[2,216,128]{2,1,0:...) custom-call(f32[1]{0:T(128)S(6)} %copy.18.depth_ref, ...), custom_call_target="tpu_custom_call" | custom-call | tf_op jit(solution)/shard_map/front/pallas_call | solution.py:514
  8.6 3.5 %second.1 = bf16[16,168,128]{2,1,0:T(8,128)(2,1)} custom-call(f32[1]{0:T(128)S(6)} %copy.18.depth_ref, f32[1,128]{1,0:T(1,128)S(1)} %get-tuple-element.22.energy_ref, bf16[648,1024]{1,0:T(8,128)(2,1)S(1)} %get-tuple-element.23.sum_ref, bf16[768,672]{1,0:T(8,128)(2,1)S(1)} %get-tuple-element.24.place_ref, bf16[672,648]{1,0:T(8,128)(2,1)S(1)} %get-tuple-element.25.wave_ref, ...), custom_call_target="tpu_custom_call" | custom-call | tf_op jit(solution)/shard_map/second/pallas_call | solution.py:559
  12.1 0.0 copy-start.1
  12.1 0.0 copy-start.2
  12.1 0.0 copy-start.3
  12.1 0.0 copy-start.4
  12.1 0.0 copy-start.6
  12.1 6.7 %all-to-all-start = ((bf16[16,168,128]{2,1,0:T(8,128)(2,1)}), bf16[16,168,128]{2,1,0:T(8,128)(2,1)S(1)}, u32[]{:S(2)}, u32[]{:S(2)}) async-start(bf16[16,168,128]{2,1,0:T(8,128)(2,1)} %second.1), calls=%async_computation | async-start | bytes 1376256 | tf_op jit(solution)/shard_map/all_to_all | solution.py:560
  18.8 1.2 %collective-permute-start = (bf16[2,216,128]{2,1,0:T(8,128)(2,1)S(1)}, bf16[2,216,128]{2,1,0:T(8,128)(2,1)S(1)}, u32[]{:S(2)}, u32[]{:S(2)}) collective-permute-start(bf16[2,216,128]{2,1,0:T(8,128)(2,1)S(1)} %get-tuple-element.29), channel_id=1, source_target_pairs={{0,2},{1,3},{2,0},{3,1},{4,6},{5,7},{6,4},{7,5},{8,10},{9,11},{10,... | collective-permute-start | bytes 331784 | tf_op jit(solution)/shard_map/ppermute | solution.py:543
  20.0 1.2 %collective-permute-start.1 = (bf16[2,216,128]{2,1,0:T(8,128)(2,1)S(1)}, bf16[2,216,128]{2,1,0:T(8,128)(2,1)S(1)}, u32[]{:S(2)}, u32[]{:S(2)}) collective-permute-start(bf16[2,216,128]{2,1,0:T(8,128)(2,1)S(1)} %get-tuple-element.30), channel_id=1, source_target_pairs={{0,4},{1,5},{2,6},{3,7},{4,8},{5,9},{6,10},{7,11},{8,12},{9,13},{1... | collective-permute-start | bytes 331784 | tf_op jit(solution)/shard_map/ppermute | solution.py:543
  21.2 1.2 %collective-permute-start.2 = (bf16[2,216,128]{2,1,0:T(8,128)(2,1)S(1)}, bf16[2,216,128]{2,1,0:T(8,128)(2,1)S(1)}, u32[]{:S(2)}, u32[]{:S(2)}) collective-permute-start(bf16[2,216,128]{2,1,0:T(8,128)(2,1)S(1)} %get-tuple-element.31), channel_id=1, source_target_pairs={{0,6},{1,7},{2,4},{3,5},{4,10},{5,11},{6,8},{7,9},{8,14},{9,15},{1... | collective-permute-start | bytes 331784 | tf_op jit(solution)/shard_map/ppermute | solution.py:543
  22.4 1.2 %collective-permute-start.3 = (bf16[2,216,128]{2,1,0:T(8,128)(2,1)S(1)}, bf16[2,216,128]{2,1,0:T(8,128)(2,1)S(1)}, u32[]{:S(2)}, u32[]{:S(2)}) collective-permute-start(bf16[2,216,128]{2,1,0:T(8,128)(2,1)S(1)} %get-tuple-element.32), channel_id=1, source_target_pairs={{0,8},{1,9},{2,10},{3,11},{4,12},{5,13},{6,14},{7,15},{8,0},{9,1},... | collective-permute-start | bytes 331784 | tf_op jit(solution)/shard_map/ppermute | solution.py:543
  23.6 2.1 %collective-permute-start.4 = (bf16[2,216,128]{2,1,0:T(8,128)(2,1)S(1)}, bf16[2,216,128]{2,1,0:T(8,128)(2,1)S(1)}, u32[]{:S(2)}, u32[]{:S(2)}) collective-permute-start(bf16[2,216,128]{2,1,0:T(8,128)(2,1)S(1)} %get-tuple-element.33), channel_id=1, source_target_pairs={{0,10},{1,11},{2,8},{3,9},{4,14},{5,15},{6,12},{7,13},{8,2},{9,3},... | collective-permute-start | bytes 331784 | tf_op jit(solution)/shard_map/ppermute | solution.py:543
  25.6 0.9 %collective-permute-done.refs_1_ = bf16[2,216,128]{2,1,0:T(8,128)(2,1)S(1)} collective-permute-done((bf16[2,216,128]{2,1,0:T(8,128)(2,1)S(1)}, bf16[2,216,128]{2,1,0:T(8,128)(2,1)S(1)}, u32[]{:S(2)}, u32[]{:S(2)}) %collective-permute-start) | collective-permute-done | bytes 110624 | tf_op jit(solution)/shard_map/ppermute | solution.py:543
  26.6 1.4 %collective-permute-start.5 = (bf16[2,216,128]{2,1,0:T(8,128)(2,1)S(1)}, bf16[2,216,128]{2,1,0:T(8,128)(2,1)S(1)}, u32[]{:S(2)}, u32[]{:S(2)}) collective-permute-start(bf16[2,216,128]{2,1,0:T(8,128)(2,1)S(1)} %get-tuple-element.34), channel_id=1, source_target_pairs={{0,12},{1,13},{2,14},{3,15},{4,0},{5,1},{6,2},{7,3},{8,4},{9,5},{1... | collective-permute-start | bytes 331784 | tf_op jit(solution)/shard_map/ppermute | solution.py:543
  27.9 17.7 %collective-permute-done.1.refs_2_ = bf16[2,216,128]{2,1,0:T(8,128)(2,1)S(1)} collective-permute-done((bf16[2,216,128]{2,1,0:T(8,128)(2,1)S(1)}, bf16[2,216,128]{2,1,0:T(8,128)(2,1)S(1)}, u32[]{:S(2)}, u32[]{:S(2)}) %collective-permute-start.1) | collective-permute-done | bytes 110624 | tf_op jit(solution)/shard_map/ppermute | solution.py:543
  45.6 0.0 collective-permute-start.6
  45.6 2.4 %collective-permute-done.2.refs_3_ = bf16[2,216,128]{2,1,0:T(8,128)(2,1)S(1)} collective-permute-done((bf16[2,216,128]{2,1,0:T(8,128)(2,1)S(1)}, bf16[2,216,128]{2,1,0:T(8,128)(2,1)S(1)}, u32[]{:S(2)}, u32[]{:S(2)}) %collective-permute-start.2) | collective-permute-done | bytes 110624 | tf_op jit(solution)/shard_map/ppermute | solution.py:543
  48.0 2.4 %collective-permute-done.3.refs_4_ = bf16[2,216,128]{2,1,0:T(8,128)(2,1)S(1)} collective-permute-done((bf16[2,216,128]{2,1,0:T(8,128)(2,1)S(1)}, bf16[2,216,128]{2,1,0:T(8,128)(2,1)S(1)}, u32[]{:S(2)}, u32[]{:S(2)}) %collective-permute-start.3) | collective-permute-done | bytes 110624 | tf_op jit(solution)/shard_map/ppermute | solution.py:543
  50.4 2.4 %collective-permute-done.4.refs_5_ = bf16[2,216,128]{2,1,0:T(8,128)(2,1)S(1)} collective-permute-done((bf16[2,216,128]{2,1,0:T(8,128)(2,1)S(1)}, bf16[2,216,128]{2,1,0:T(8,128)(2,1)S(1)}, u32[]{:S(2)}, u32[]{:S(2)}) %collective-permute-start.4) | collective-permute-done | bytes 110624 | tf_op jit(solution)/shard_map/ppermute | solution.py:543
  52.7 0.0 collective-permute-done.5.refs_6_
  52.7 2.8 %collective-permute-done.6.refs_7_ = bf16[2,216,128]{2,1,0:T(8,128)(2,1)S(1)} collective-permute-done((bf16[2,216,128]{2,1,0:T(8,128)(2,1)S(1)}, bf16[2,216,128]{2,1,0:T(8,128)(2,1)S(1)}, u32[]{:S(2)}, u32[]{:S(2)}) %collective-permute-start.6) | collective-permute-done | bytes 110624 | tf_op jit(solution)/shard_map/ppermute | solution.py:543
  55.6 0.0 copy-start.5
  55.6 1.0 %collective-permute-start.7 = (bf16[8,216,128]{2,1,0:T(8,128)(2,1)S(1)}, bf16[8,216,128]{2,1,0:T(8,128)(2,1)S(1)}, u32[]{:S(2)}, u32[]{:S(2)}) collective-permute-start(bf16[8,216,128]{2,1,0:T(8,128)(2,1)S(1)} %repack.1), channel_id=1, source_target_pairs={{0,1},{1,0},{2,3},{3,2},{4,5},{5,4},{6,7},{7,6},{8,9},{9,8},{10,11... | collective-permute-start | bytes 1327112 | tf_op jit(solution)/shard_map/ppermute | solution.py:571
  56.7 1.4 %collective-permute-done.7.refs_8_ = bf16[8,216,128]{2,1,0:T(8,128)(2,1)S(1)} collective-permute-done((bf16[8,216,128]{2,1,0:T(8,128)(2,1)S(1)}, bf16[8,216,128]{2,1,0:T(8,128)(2,1)S(1)}, u32[]{:S(2)}, u32[]{:S(2)}) %collective-permute-start.7) | collective-permute-done | bytes 442400 | tf_op jit(solution)/shard_map/ppermute | solution.py:571
  58.1 0.0 copy-done.1
  58.1 0.0 copy-done.2
  58.1 0.0 copy-done.3
  58.1 0.0 copy-done.4
  58.1 0.0 copy-done.6
  58.1 4.2 %odd.1 = (f32[672,1024]{1,0:T(8,128)S(1)}, bf16[512,256]{1,0:T(8,128)(2,1)S(1)}, bf16[672,128]{1,0:T(8,128)(2,1)S(1)}) custom-call(s32[16]{0:T(128)S(1)} %copy-done.6, bf16[512,256]{1,0:T(8,128)(2,1)S(1)} %copy-done.3, bf16[128,256]{1,0:T(8,128)(2,1)S(1)} %copy-done.2, f32[32,640]{1,0:T(8,128)S(1)} %copy-done.4, bf16[640,1024]{1,0:T(8,128)(2,1)S(1)} %copy-done.1, ...), custom_call_target="tpu_custom_call" | custom-call | tf_op jit(solution)/shard_map/odd/pallas_call | solution.py:577
  62.3 0.0 copy-start
  62.3 1.5 %copy-done = f32[672,1024]{1,0:T(8,128)} copy-done((f32[672,1024]{1,0:T(8,128)}, f32[672,1024]{1,0:T(8,128)S(1)}, u32[]{:S(2)}) %copy-start) | copy-done | bytes 2752536
  63.9 0.0 all-to-all-done.arrived_hbm
  63.9 0.0 copy-start.7
  63.9 0.8 %copy-done.7 = bf16[16,168,128]{2,1,0:T(8,128)(2,1)} copy-done((bf16[16,168,128]{2,1,0:T(8,128)(2,1)}, bf16[16,168,128]{2,1,0:T(8,128)(2,1)S(1)}, u32[]{:S(2)}) %copy-start.7) | copy-done | bytes 688152
  64.7 0.0 copy-done.5
  64.7 5.3 %last.1 = f32[672,2048]{1,0:T(8,128)} custom-call(bf16[16,168,128]{2,1,0:T(8,128)(2,1)} %copy-done.7, bf16[512,256]{1,0:T(8,128)(2,1)S(1)} %get-tuple-element.36.forward_hbm, bf16[128,256]{1,0:T(8,128)(2,1)S(1)} %copy-done.2, f32[32,512]{1,0:T(8,128)S(1)} %copy-done.5, bf16[672,128]{1,0:T(8,128)(2,1)S(1)} %get-tuple-element.37.mixed_hbm, ...), custom_call_target="tpu_custom_call" | custom-call | tf_op jit(solution)/shard_map/last/pallas_call | solution.py:600
  (1 shorter events, 0.0 us)
Async XLA Ops:
  12.1 46.0 %copy-start.1 = (bf16[640,1024]{1,0:T(8,128)(2,1)S(1)}, bf16[640,1024]{1,0:T(8,128)(2,1)}, u32[]{:S(2)}) copy-start(bf16[640,1024]{1,0:T(8,128)(2,1)} %constant.33.clone.table_hbm) | copy-start | bytes 3932164
  12.1 46.0 %copy-start.2 = (bf16[128,256]{1,0:T(8,128)(2,1)S(1)}, bf16[128,256]{1,0:T(8,128)(2,1)}, u32[]{:S(2)}) copy-start(bf16[128,256]{1,0:T(8,128)(2,1)} %constant.31.clone.inverse_hbm) | copy-start | bytes 196612
  12.1 46.0 %copy-start.3 = (bf16[512,256]{1,0:T(8,128)(2,1)S(1)}, bf16[512,256]{1,0:T(8,128)(2,1)}, u32[]{:S(2)}) copy-start(bf16[512,256]{1,0:T(8,128)(2,1)} %constant.30.clone.forward_hbm) | copy-start | bytes 786436
  12.1 46.0 %copy-start.4 = (f32[32,640]{1,0:T(8,128)S(1)}, f32[32,640]{1,0:T(8,128)}, u32[]{:S(2)}) copy-start(f32[32,640]{1,0:T(8,128)} %constant.32.clone.response_hbm) | copy-start | bytes 245764
  12.1 46.0 %copy-start.6 = (s32[16]{0:T(128)S(1)}, s32[16]{0:T(128)}, u32[]{:S(2)}) copy-start(s32[16]{0:T(128)} %slot_ref.1) | copy-start | bytes 196
  12.1 51.8 %all-to-all-start = ((bf16[16,168,128]{2,1,0:T(8,128)(2,1)}), bf16[16,168,128]{2,1,0:T(8,128)(2,1)S(1)}, u32[]{:S(2)}, u32[]{:S(2)}) async-start(bf16[16,168,128]{2,1,0:T(8,128)(2,1)} %second.1), calls=%async_computation | async-start | bytes 1376256 | tf_op jit(solution)/shard_map/all_to_all | solution.py:560
  18.8 7.7 %collective-permute-start = (bf16[2,216,128]{2,1,0:T(8,128)(2,1)S(1)}, bf16[2,216,128]{2,1,0:T(8,128)(2,1)S(1)}, u32[]{:S(2)}, u32[]{:S(2)}) collective-permute-start(bf16[2,216,128]{2,1,0:T(8,128)(2,1)S(1)} %get-tuple-element.29), channel_id=1, source_target_pairs={{0,2},{1,3},{2,0},{3,1},{4,6},{5,7},{6,4},{7,5},{8,10},{9,11},{10,... | collective-permute-start | bytes 331784 | tf_op jit(solution)/shard_map/ppermute | solution.py:543
  20.0 25.6 %collective-permute-start.1 = (bf16[2,216,128]{2,1,0:T(8,128)(2,1)S(1)}, bf16[2,216,128]{2,1,0:T(8,128)(2,1)S(1)}, u32[]{:S(2)}, u32[]{:S(2)}) collective-permute-start(bf16[2,216,128]{2,1,0:T(8,128)(2,1)S(1)} %get-tuple-element.30), channel_id=1, source_target_pairs={{0,4},{1,5},{2,6},{3,7},{4,8},{5,9},{6,10},{7,11},{8,12},{9,13},{1... | collective-permute-start | bytes 331784 | tf_op jit(solution)/shard_map/ppermute | solution.py:543
  21.2 26.8 %collective-permute-start.2 = (bf16[2,216,128]{2,1,0:T(8,128)(2,1)S(1)}, bf16[2,216,128]{2,1,0:T(8,128)(2,1)S(1)}, u32[]{:S(2)}, u32[]{:S(2)}) collective-permute-start(bf16[2,216,128]{2,1,0:T(8,128)(2,1)S(1)} %get-tuple-element.31), channel_id=1, source_target_pairs={{0,6},{1,7},{2,4},{3,5},{4,10},{5,11},{6,8},{7,9},{8,14},{9,15},{1... | collective-permute-start | bytes 331784 | tf_op jit(solution)/shard_map/ppermute | solution.py:543
  22.4 28.0 %collective-permute-start.3 = (bf16[2,216,128]{2,1,0:T(8,128)(2,1)S(1)}, bf16[2,216,128]{2,1,0:T(8,128)(2,1)S(1)}, u32[]{:S(2)}, u32[]{:S(2)}) collective-permute-start(bf16[2,216,128]{2,1,0:T(8,128)(2,1)S(1)} %get-tuple-element.32), channel_id=1, source_target_pairs={{0,8},{1,9},{2,10},{3,11},{4,12},{5,13},{6,14},{7,15},{8,0},{9,1},... | collective-permute-start | bytes 331784 | tf_op jit(solution)/shard_map/ppermute | solution.py:543
  23.6 29.2 %collective-permute-start.4 = (bf16[2,216,128]{2,1,0:T(8,128)(2,1)S(1)}, bf16[2,216,128]{2,1,0:T(8,128)(2,1)S(1)}, u32[]{:S(2)}, u32[]{:S(2)}) collective-permute-start(bf16[2,216,128]{2,1,0:T(8,128)(2,1)S(1)} %get-tuple-element.33), channel_id=1, source_target_pairs={{0,10},{1,11},{2,8},{3,9},{4,14},{5,15},{6,12},{7,13},{8,2},{9,3},... | collective-permute-start | bytes 331784 | tf_op jit(solution)/shard_map/ppermute | solution.py:543
  26.6 26.2 %collective-permute-start.5 = (bf16[2,216,128]{2,1,0:T(8,128)(2,1)S(1)}, bf16[2,216,128]{2,1,0:T(8,128)(2,1)S(1)}, u32[]{:S(2)}, u32[]{:S(2)}) collective-permute-start(bf16[2,216,128]{2,1,0:T(8,128)(2,1)S(1)} %get-tuple-element.34), channel_id=1, source_target_pairs={{0,12},{1,13},{2,14},{3,15},{4,0},{5,1},{6,2},{7,3},{8,4},{9,5},{1... | collective-permute-start | bytes 331784 | tf_op jit(solution)/shard_map/ppermute | solution.py:543
  45.6 9.9 %collective-permute-start.6 = (bf16[2,216,128]{2,1,0:T(8,128)(2,1)S(1)}, bf16[2,216,128]{2,1,0:T(8,128)(2,1)S(1)}, u32[]{:S(2)}, u32[]{:S(2)}) collective-permute-start(bf16[2,216,128]{2,1,0:T(8,128)(2,1)S(1)} %get-tuple-element.35), channel_id=1, source_target_pairs={{0,14},{1,15},{2,12},{3,13},{4,2},{5,3},{6,0},{7,1},{8,6},{9,7},{1... | collective-permute-start | bytes 331784 | tf_op jit(solution)/shard_map/ppermute | solution.py:543
  55.6 9.1 %copy-start.5 = (f32[32,512]{1,0:T(8,128)S(1)}, f32[32,512]{1,0:T(8,128)}, u32[]{:S(2)}) copy-start(f32[32,512]{1,0:T(8,128)} %constant.34.clone.response_hbm) | copy-start | bytes 196612
  55.6 2.5 %collective-permute-start.7 = (bf16[8,216,128]{2,1,0:T(8,128)(2,1)S(1)}, bf16[8,216,128]{2,1,0:T(8,128)(2,1)S(1)}, u32[]{:S(2)}, u32[]{:S(2)}) collective-permute-start(bf16[8,216,128]{2,1,0:T(8,128)(2,1)S(1)} %repack.1), channel_id=1, source_target_pairs={{0,1},{1,0},{2,3},{3,2},{4,5},{5,4},{6,7},{7,6},{8,9},{9,8},{10,11... | collective-permute-start | bytes 1327112 | tf_op jit(solution)/shard_map/ppermute | solution.py:571
  62.3 1.6 %copy-start = (f32[672,1024]{1,0:T(8,128)}, f32[672,1024]{1,0:T(8,128)S(1)}, u32[]{:S(2)}) copy-start(f32[672,1024]{1,0:T(8,128)S(1)} %get-tuple-element.38.odd_hbm) | copy-start | bytes 8257540
  63.9 0.8 %copy-start.7 = (bf16[16,168,128]{2,1,0:T(8,128)(2,1)}, bf16[16,168,128]{2,1,0:T(8,128)(2,1)S(1)}, u32[]{:S(2)}) copy-start(bf16[16,168,128]{2,1,0:T(8,128)(2,1)S(1)} %all-to-all-done.arrived_hbm) | copy-start | bytes 2064388

commit v3 on v2

--- a/solution.py
+++ b/solution.py
@@ -214,6 +214,8 @@
         self.shared = UNIT // self.left if self.left else 1
         self.left_units = -(-tiles // self.shared) if self.left else 0
         self.units = self.whole * tiles + self.left_units
+        self.packed = self.whole > 0 and self.left > 0 and UNIT % self.left == 0
+        self.frame = self.whole * UNIT if self.packed else -(-per // UNIT) * UNIT
 
     def unit(self, tile, u):
         if u < self.whole:
@@ -233,7 +235,8 @@
     return [2 * dz + dx for dz in far for dx in range(2)] + [1]
 
 
-def place_message(placed, layout, frame, store, i, energy=None):
+def place_message(placed, layout, store, i, records, energy=None):
+    frame = layout.frame
     mine = placed[i * frame : (i + 1) * frame]
     if energy is not None:
         top = jnp.concatenate([with_energy(mine[:UNIT, :LANES], energy), mine[:UNIT, LANES:]], axis=1)
@@ -242,11 +245,17 @@
     left = [jnp.zeros((UNIT, LANES), F32) for _ in range(layout.left_units)]
     if layout.left:
         row = lax.broadcasted_iota(jnp.int32, (UNIT, LANES), 0)
+        if layout.packed:
+            at = records * frame + i * layout.left // UNIT * UNIT
+            last, off = placed[at : at + UNIT], i * layout.left % UNIT
+        else:
+            last, off = mine[layout.whole * UNIT : (layout.whole + 1) * UNIT], 0
         for t in range(layout.tiles):
-            unit = mine[layout.whole * UNIT : (layout.whole + 1) * UNIT, t * LANES : (t + 1) * LANES]
             shift = t % layout.shared * layout.left
-            unit = jnp.where(row < layout.left, unit, 0.0)
-            left[t // layout.shared] += pltpu.roll(unit, shift, 0) if shift else unit
+            unit = last[:, t * LANES : (t + 1) * LANES]
+            move = (shift - off) % UNIT
+            unit = pltpu.roll(unit, move, 0) if move else unit
+            left[t // layout.shared] += jnp.where((row >= shift) & (row < shift + layout.left), unit, 0.0)
     store(jnp.concatenate(parts + left, axis=0).astype(BF))
 
 
@@ -281,7 +290,7 @@
     return copies
 
 
-def front_kernel(per, frame, layout, records, count):
+def front_kernel(per, rows, layout, records, count):
     def kernel(depth_ref, receiver_ref, home_ref, vertical_hbm, wave_hbm, traces_hbm, table_hbm, mixed_hbm, *refs):
         later_hbm = refs[:2]
         *messages, sum_ref, place_ref, wave_ref, energy_ref = refs[2 : 6 + count]
@@ -301,12 +310,17 @@
         n = records // 4
         turn = (device >> 2) - me // 4
         turn = jnp.where(turn < 0, turn + n, turn)
-        home_row = (turn * 4 + ((device & 3) ^ (me % 4))) * frame + (home - device * per)
+        turn = turn * 4 + ((device & 3) ^ (me % 4))
+        slot = home - device * per
+        frame = layout.frame
+        home_row = turn * frame + slot
+        if layout.packed:
+            home_row = jnp.where(slot < frame, home_row, records * frame + turn * layout.left + slot - frame)
         both = jnp.concatenate([home_row >> 7, home_row & 127, jnp.zeros((14, n_rec), jnp.int32)], axis=0).astype(F32).astype(BF)
         to_bin = lax.broadcasted_iota(jnp.int32, (n_rec, n_channels), 0) == receiver_ref[...].reshape(1, n_channels)
         target = dot(both, jnp.where(to_bin, 1.0, 0.0).astype(BF))
         target = (target[0:1] * 128.0 + target[1:2]).astype(jnp.int32)
-        picked = lax.broadcasted_iota(jnp.int32, (records * frame, n_channels), 0) == target
+        picked = lax.broadcasted_iota(jnp.int32, (rows, n_channels), 0) == target
         picked = jnp.where(picked, 1.0, 0.0).astype(BF)
         copies[0].wait()
         place_ref[...] = lax.dot_general(picked, wave_ref[...], (((1,), (1,)), ((), ())), preferred_element_type=F32).astype(BF)
@@ -333,14 +347,14 @@
         energy_ref[...] = energy_of(placed_ref[...])
         for i in range(records):
             store = into(messages[0], partner(me, i // 4, i % 4, n, 1)) if count == 1 else into(messages[i // 2], i % 2)
-            place_message(placed_ref, layout, frame, store, i)
+            place_message(placed_ref, layout, store, i, records)
         for c in outs:
             c.wait()
 
     return kernel
 
 
-def second_kernel(frame, layout, records):
+def second_kernel(layout, records):
     def kernel(depth_ref, energy_ref, sum_ref, place_ref, wave_ref, table_ref, vertical_ref, message_ref, placed_ref, factors_ref):
         me = lax.axis_index("shard")
         store_factors(factors_ref, vertical_ref, depth_ref[0], sum_ref.shape[0])
@@ -349,7 +363,7 @@
         pieces = split_energy(energy_ref[...] + energy_of(placed_ref[...]))
         for i in range(records):
             store = into(message_ref, partner(me, i // 4, i % 4, records // 4, 1))
-            place_message(placed_ref, layout, frame, store, i, pieces)
+            place_message(placed_ref, layout, store, i, records, pieces)
 
     return kernel
 
@@ -427,7 +441,7 @@
         filter_gathers(arrived, layout, forward_ref, inverse_ref, response_ref, filtered_ref, per, block)
         mixed = filtered_ref.at[:, pl.ds((layout.tiles - 1) * LANES, LANES)]
         outs = start_all([(forward_b_ref, forward_b_hbm), (mixed, mixed_hbm)], sems, 4)
-        out_ref[...] = dot(filtered_ref[...], table_ref[...])
+        out_ref[...] = dot(filtered_ref[...], table_ref[...]).astype(BF)
         for c in outs + start_all([(out_ref, out_hbm)], sems, 6):
             c.wait()
 
@@ -465,7 +479,7 @@
             fours = dot(jnp.concatenate([filtered_ref[here, : whole // 2], left], axis=1), table_ref[0])
             twos = dot(jnp.concatenate([filtered_ref[here, whole // 2 : whole], left], axis=1), table_ref[1])
             for q, even in enumerate((fours + twos, fours - twos)):
-                odd = odd_ref[here, q * quarter : (q + 1) * quarter]
+                odd = odd_ref[here, q * quarter : (q + 1) * quarter].astype(F32)
                 for p, value in enumerate((even + odd, even - odd)):
                     there = pl.ds((2 * p + q) * quarter, quarter)
                     out_ref[here, there] = value * scale
@@ -483,11 +497,11 @@
     n_channels, n_samples = traces.shape
     half = n_samples // 2
     block = 2 * UNIT if records <= 16 else UNIT
-    frame = -(-per // UNIT) * UNIT
     even_tiles, odd_tiles, mixed = bin_tiles()
     n_whole = len(even_tiles)
     layout = Layout(per, n_whole + 1)
     layout_b = Layout(per, n_whole)
+    rows = records * (per if layout.packed else layout.frame)
     wave = wave_table(n_channels)
     odd_table = time_table(n_samples, odd_tiles + [mixed], 1)
     even_whole = time_table(n_samples, even_tiles, 0)
@@ -512,11 +526,11 @@
     planes = records // 2 if pairwise else 1
     made = pltpu.VMEM if pairwise else jax.ShapeDtypeStruct
     *sources, sums, place, wave_kept, energy, even_kept, vertical_kept = pl.pallas_call(
-        front_kernel(per, frame, layout, records, planes),
+        front_kernel(per, rows, layout, records, planes),
         out_shape=(
             *(made((records // planes, layout.units * UNIT, LANES), BF) for _ in range(planes)),
             pltpu.VMEM((n_channels, half), BF),
-            pltpu.VMEM((records * frame, wave.shape[0]), BF),
+            pltpu.VMEM((rows, wave.shape[0]), BF),
             scratch(wave),
             pltpu.VMEM((1, LANES), F32),
             scratch(even_whole),
@@ -530,7 +544,7 @@
             scratch(odd_table),
             scratch(mixed_even),
             pltpu.VMEM((n_channels, half), BF),
-            pltpu.VMEM((records * frame, (n_whole + 1) * LANES), F32),
+            pltpu.VMEM((rows, (n_whole + 1) * LANES), F32),
             pltpu.VMEM((2, n_whole + 1, wave.shape[0] // 2, LANES), F32),
             pltpu.SemaphoreType.DMA((10,)),
         ],
@@ -545,12 +559,12 @@
         sources = [lax.all_to_all(sources[0], "shard", split_axis=0, concat_axis=0, tiled=True)]
 
     second = pl.pallas_call(
-        second_kernel(frame, layout_b, records),
+        second_kernel(layout_b, records),
         out_shape=jax.ShapeDtypeStruct((records, layout_b.units * UNIT, LANES), BF),
         in_specs=[smem] + [vmem] * 6,
         out_specs=vmem,
         scratch_shapes=[
-            pltpu.VMEM((records * frame, n_whole * LANES), F32),
+            pltpu.VMEM((rows, n_whole * LANES), F32),
             pltpu.VMEM((2, n_whole, wave.shape[0] // 2, LANES), F32),
         ],
         compiler_params=shared,
@@ -577,14 +591,14 @@
     odd, forward_b, mixed_part = pl.pallas_call(
         odd_kernel(per, block, layout, records, len(sources)),
         out_shape=(
-            jax.ShapeDtypeStruct((per * records, half), F32),
+            jax.ShapeDtypeStruct((per * records, half), BF),
             jax.ShapeDtypeStruct(forward.shape, BF),
             jax.ShapeDtypeStruct((per * records, LANES), BF),
         ),
         in_specs=[smem] + [hbm] * 4 + [vmem] * len(sources),
         out_specs=(hbm,) * 3,
         scratch_shapes=[
-            pltpu.VMEM((per * records, half), F32),
+            pltpu.VMEM((per * records, half), BF),
             scratch(forward),
             scratch(forward),
             scratch(forward),
@@ -608,7 +622,7 @@
             scratch(inverse),
             pltpu.VMEM((2 * records, n_whole * LANES), F32),
             scratch(back_table),
-            pltpu.VMEM((per * records, half), F32),
+            pltpu.VMEM((per * records, half), BF),
             pltpu.VMEM((per * records, (n_whole + 1) * LANES), BF),
             pltpu.VMEM((per * records, n_samples), F32),
             pltpu.SemaphoreType.DMA((6 + 5 * -(-per // block),)),

time: 70.4 us -> 69.6 us (0.989)
  no operation moved by 1% of the time
where the time goes in v3:
time: 69.6 us; the launch traced here: 69.4 us
  waiting for transfers between devices  30 us (43%)
  Pallas kernels  20.6 us (30%)
  starting transfers between devices  15.9 us (23%)
  local copies, waits for them, and re-layouts  1.98 us (3%)
  between operations  0.89 us (1%)
    ppermute x7, waiting for transfers between devices, shards(): sources[chip] = lax.ppermute(sources[chip], 'shard', route)  28.5 us
    ppermute x7, starting transfers between devices, shards(): sources[chip] = lax.ppermute(sources[chip], 'shard', route)  8.2 us
    pallas_call x1, Pallas kernels, shards(): pl.pallas_call(front_kernel(per, rows, layout, records, planes), out_shap...  7.81 us
    all_to_all x1, starting transfers between devices, shards(): lax.all_to_all(message_b, 'shard', split_axis=0, concat_axis=0, tiled=True)  6.7 us
    pallas_call x1, Pallas kernels, shards(): pl.pallas_call(last_kernel(per, block, layout_b, n_channels * records, re...  5.21 us
    pallas_call x1, Pallas kernels, shards(): pl.pallas_call(odd_kernel(per, block, layout, records, len(sources)), out...  4.04 us
    pallas_call x1, Pallas kernels, shards(): second(cable_depth, energy, sums, place, wave_kept, even_kept, vertical_k...  3.49 us
    unnamed x16, local copies, waits for them, and re-layouts  1.98 us
  transfers between devices with their start and end apart: 9, of which 7 were waited for; matrix products, arithmetic and copies ran while one was open for 0% of the time, Pallas kernels for 6%

profile of v3, /device:TPU:9, one launch (start us, length us, event | category | flops | bytes accessed | tf_op | source)
XLA Modules:
  0.0 69.4 jit_solution(4188145367427002981)
XLA Ops:
  0.7 7.8 %front.1 = (bf16[2,216,128]{2,1,0:T(8,128)(2,1)S(1)}, bf16[2,216,128]{2,1,0:T(8,128)(2,1)S(1)}, bf16[2,216,128]{2,1,0:T(8,128)(2,1)S(1)}, bf16[2,216,128]{2,1,0:...) custom-call(f32[1]{0:T(128)S(6)} %copy.18.depth_ref, ...), custom_call_target="tpu_custom_call" | custom-call | tf_op jit(solution)/shard_map/front/pallas_call | solution.py:528
  8.5 3.5 %second.1 = bf16[16,168,128]{2,1,0:T(8,128)(2,1)} custom-call(f32[1]{0:T(128)S(6)} %copy.18.depth_ref, f32[1,128]{1,0:T(1,128)S(1)} %get-tuple-element.22.energy_ref, bf16[648,1024]{1,0:T(8,128)(2,1)S(1)} %get-tuple-element.23.sum_ref, bf16[672,672]{1,0:T(8,128)(2,1)S(1)} %get-tuple-element.24.place_ref, bf16[672,648]{1,0:T(8,128)(2,1)S(1)} %get-tuple-element.25.wave_ref, ...), custom_call_target="tpu_custom_call" | custom-call | tf_op jit(solution)/shard_map/second/pallas_call | solution.py:573
  12.0 0.0 copy-start.1
  12.0 0.0 copy-start.2
  12.0 0.0 copy-start.3
  12.0 0.0 copy-start.4
  12.0 0.0 copy-start.6
  12.0 6.7 %all-to-all-start = ((bf16[16,168,128]{2,1,0:T(8,128)(2,1)}), bf16[16,168,128]{2,1,0:T(8,128)(2,1)S(1)}, u32[]{:S(2)}, u32[]{:S(2)}) async-start(bf16[16,168,128]{2,1,0:T(8,128)(2,1)} %second.1), calls=%async_computation | async-start | bytes 1376256 | tf_op jit(solution)/shard_map/all_to_all | solution.py:574
  18.7 1.2 %collective-permute-start = (bf16[2,216,128]{2,1,0:T(8,128)(2,1)S(1)}, bf16[2,216,128]{2,1,0:T(8,128)(2,1)S(1)}, u32[]{:S(2)}, u32[]{:S(2)}) collective-permute-start(bf16[2,216,128]{2,1,0:T(8,128)(2,1)S(1)} %get-tuple-element.29), channel_id=1, source_target_pairs={{0,2},{1,3},{2,0},{3,1},{4,6},{5,7},{6,4},{7,5},{8,10},{9,11},{10,... | collective-permute-start | bytes 331784 | tf_op jit(solution)/shard_map/ppermute | solution.py:557
  19.9 1.2 %collective-permute-start.1 = (bf16[2,216,128]{2,1,0:T(8,128)(2,1)S(1)}, bf16[2,216,128]{2,1,0:T(8,128)(2,1)S(1)}, u32[]{:S(2)}, u32[]{:S(2)}) collective-permute-start(bf16[2,216,128]{2,1,0:T(8,128)(2,1)S(1)} %get-tuple-element.30), channel_id=1, source_target_pairs={{0,4},{1,5},{2,6},{3,7},{4,8},{5,9},{6,10},{7,11},{8,12},{9,13},{1... | collective-permute-start | bytes 331784 | tf_op jit(solution)/shard_map/ppermute | solution.py:557
  21.1 1.2 %collective-permute-start.2 = (bf16[2,216,128]{2,1,0:T(8,128)(2,1)S(1)}, bf16[2,216,128]{2,1,0:T(8,128)(2,1)S(1)}, u32[]{:S(2)}, u32[]{:S(2)}) collective-permute-start(bf16[2,216,128]{2,1,0:T(8,128)(2,1)S(1)} %get-tuple-element.31), channel_id=1, source_target_pairs={{0,6},{1,7},{2,4},{3,5},{4,10},{5,11},{6,8},{7,9},{8,14},{9,15},{1... | collective-permute-start | bytes 331784 | tf_op jit(solution)/shard_map/ppermute | solution.py:557
  22.2 1.2 %collective-permute-start.3 = (bf16[2,216,128]{2,1,0:T(8,128)(2,1)S(1)}, bf16[2,216,128]{2,1,0:T(8,128)(2,1)S(1)}, u32[]{:S(2)}, u32[]{:S(2)}) collective-permute-start(bf16[2,216,128]{2,1,0:T(8,128)(2,1)S(1)} %get-tuple-element.32), channel_id=1, source_target_pairs={{0,8},{1,9},{2,10},{3,11},{4,12},{5,13},{6,14},{7,15},{8,0},{9,1},... | collective-permute-start | bytes 331784 | tf_op jit(solution)/shard_map/ppermute | solution.py:557
  23.4 2.1 %collective-permute-start.4 = (bf16[2,216,128]{2,1,0:T(8,128)(2,1)S(1)}, bf16[2,216,128]{2,1,0:T(8,128)(2,1)S(1)}, u32[]{:S(2)}, u32[]{:S(2)}) collective-permute-start(bf16[2,216,128]{2,1,0:T(8,128)(2,1)S(1)} %get-tuple-element.33), channel_id=1, source_target_pairs={{0,10},{1,11},{2,8},{3,9},{4,14},{5,15},{6,12},{7,13},{8,2},{9,3},... | collective-permute-start | bytes 331784 | tf_op jit(solution)/shard_map/ppermute | solution.py:557
  25.5 0.9 %collective-permute-done.refs_1_ = bf16[2,216,128]{2,1,0:T(8,128)(2,1)S(1)} collective-permute-done((bf16[2,216,128]{2,1,0:T(8,128)(2,1)S(1)}, bf16[2,216,128]{2,1,0:T(8,128)(2,1)S(1)}, u32[]{:S(2)}, u32[]{:S(2)}) %collective-permute-start) | collective-permute-done | bytes 110624 | tf_op jit(solution)/shard_map/ppermute | solution.py:557
  26.4 1.4 %collective-permute-start.5 = (bf16[2,216,128]{2,1,0:T(8,128)(2,1)S(1)}, bf16[2,216,128]{2,1,0:T(8,128)(2,1)S(1)}, u32[]{:S(2)}, u32[]{:S(2)}) collective-permute-start(bf16[2,216,128]{2,1,0:T(8,128)(2,1)S(1)} %get-tuple-element.34), channel_id=1, source_target_pairs={{0,12},{1,13},{2,14},{3,15},{4,0},{5,1},{6,2},{7,3},{8,4},{9,5},{1... | collective-permute-start | bytes 331784 | tf_op jit(solution)/shard_map/ppermute | solution.py:557
  27.8 17.7 %collective-permute-done.1.refs_2_ = bf16[2,216,128]{2,1,0:T(8,128)(2,1)S(1)} collective-permute-done((bf16[2,216,128]{2,1,0:T(8,128)(2,1)S(1)}, bf16[2,216,128]{2,1,0:T(8,128)(2,1)S(1)}, u32[]{:S(2)}, u32[]{:S(2)}) %collective-permute-start.1) | collective-permute-done | bytes 110624 | tf_op jit(solution)/shard_map/ppermute | solution.py:557
  45.5 0.0 collective-permute-start.6
  45.5 2.4 %collective-permute-done.2.refs_3_ = bf16[2,216,128]{2,1,0:T(8,128)(2,1)S(1)} collective-permute-done((bf16[2,216,128]{2,1,0:T(8,128)(2,1)S(1)}, bf16[2,216,128]{2,1,0:T(8,128)(2,1)S(1)}, u32[]{:S(2)}, u32[]{:S(2)}) %collective-permute-start.2) | collective-permute-done | bytes 110624 | tf_op jit(solution)/shard_map/ppermute | solution.py:557
  47.9 2.4 %collective-permute-done.3.refs_4_ = bf16[2,216,128]{2,1,0:T(8,128)(2,1)S(1)} collective-permute-done((bf16[2,216,128]{2,1,0:T(8,128)(2,1)S(1)}, bf16[2,216,128]{2,1,0:T(8,128)(2,1)S(1)}, u32[]{:S(2)}, u32[]{:S(2)}) %collective-permute-start.3) | collective-permute-done | bytes 110624 | tf_op jit(solution)/shard_map/ppermute | solution.py:557
  50.2 2.4 %collective-permute-done.4.refs_5_ = bf16[2,216,128]{2,1,0:T(8,128)(2,1)S(1)} collective-permute-done((bf16[2,216,128]{2,1,0:T(8,128)(2,1)S(1)}, bf16[2,216,128]{2,1,0:T(8,128)(2,1)S(1)}, u32[]{:S(2)}, u32[]{:S(2)}) %collective-permute-start.4) | collective-permute-done | bytes 110624 | tf_op jit(solution)/shard_map/ppermute | solution.py:557
  52.6 0.0 collective-permute-done.5.refs_6_
  52.6 2.8 %collective-permute-done.6.refs_7_ = bf16[2,216,128]{2,1,0:T(8,128)(2,1)S(1)} collective-permute-done((bf16[2,216,128]{2,1,0:T(8,128)(2,1)S(1)}, bf16[2,216,128]{2,1,0:T(8,128)(2,1)S(1)}, u32[]{:S(2)}, u32[]{:S(2)}) %collective-permute-start.6) | collective-permute-done | bytes 110624 | tf_op jit(solution)/shard_map/ppermute | solution.py:557
  55.5 0.0 copy-start.5
  55.5 1.0 %collective-permute-start.7 = (bf16[8,216,128]{2,1,0:T(8,128)(2,1)S(1)}, bf16[8,216,128]{2,1,0:T(8,128)(2,1)S(1)}, u32[]{:S(2)}, u32[]{:S(2)}) collective-permute-start(bf16[8,216,128]{2,1,0:T(8,128)(2,1)S(1)} %repack.1), channel_id=1, source_target_pairs={{0,1},{1,0},{2,3},{3,2},{4,5},{5,4},{6,7},{7,6},{8,9},{9,8},{10,11... | collective-permute-start | bytes 1327112 | tf_op jit(solution)/shard_map/ppermute | solution.py:585
  56.5 1.4 %collective-permute-done.7.refs_8_ = bf16[8,216,128]{2,1,0:T(8,128)(2,1)S(1)} collective-permute-done((bf16[8,216,128]{2,1,0:T(8,128)(2,1)S(1)}, bf16[8,216,128]{2,1,0:T(8,128)(2,1)S(1)}, u32[]{:S(2)}, u32[]{:S(2)}) %collective-permute-start.7) | collective-permute-done | bytes 442400 | tf_op jit(solution)/shard_map/ppermute | solution.py:585
  57.9 0.0 copy-done.1
  58.0 0.0 copy-done.2
  58.0 0.0 copy-done.3
  58.0 0.0 copy-done.4
  58.0 0.0 copy-done.6
  58.0 4.0 %odd.1 = (bf16[672,1024]{1,0:T(8,128)(2,1)S(1)}, bf16[512,256]{1,0:T(8,128)(2,1)S(1)}, bf16[672,128]{1,0:T(8,128)(2,1)S(1)}) custom-call(s32[16]{0:T(128)S(1)} %copy-done.6, bf16[512,256]{1,0:T(8,128)(2,1)S(1)} %copy-done.3, bf16[128,256]{1,0:T(8,128)(2,1)S(1)} %copy-done.2, f32[32,640]{1,0:T(8,128)S(1)} %copy-done.4, bf16[640,1024]{1,0:T(8,128)(2,1)S(1)} %copy-done.1, ...), custom_call_target="tpu_custom_call" | custom-call | tf_op jit(solution)/shard_map/odd/pallas_call | solution.py:591
  62.0 0.0 copy-start
  62.0 1.1 %copy-done = bf16[672,1024]{1,0:T(8,128)(2,1)} copy-done((bf16[672,1024]{1,0:T(8,128)(2,1)}, bf16[672,1024]{1,0:T(8,128)(2,1)S(1)}, u32[]{:S(2)}) %copy-start) | copy-done | bytes 1376280
  63.1 0.0 all-to-all-done.arrived_hbm
  63.1 0.0 copy-start.7
  63.1 0.9 %copy-done.7 = bf16[16,168,128]{2,1,0:T(8,128)(2,1)} copy-done((bf16[16,168,128]{2,1,0:T(8,128)(2,1)}, bf16[16,168,128]{2,1,0:T(8,128)(2,1)S(1)}, u32[]{:S(2)}) %copy-start.7) | copy-done | bytes 688152
  64.0 0.0 copy-done.5
  64.0 5.2 %last.1 = f32[672,2048]{1,0:T(8,128)} custom-call(bf16[16,168,128]{2,1,0:T(8,128)(2,1)} %copy-done.7, bf16[512,256]{1,0:T(8,128)(2,1)S(1)} %get-tuple-element.36.forward_hbm, bf16[128,256]{1,0:T(8,128)(2,1)S(1)} %copy-done.2, f32[32,512]{1,0:T(8,128)S(1)} %copy-done.5, bf16[672,128]{1,0:T(8,128)(2,1)S(1)} %get-tuple-element.37.mixed_hbm, ...), custom_call_target="tpu_custom_call" | custom-call | tf_op jit(solution)/shard_map/last/pallas_call | solution.py:614
  (1 shorter events, 0.0 us)
Async XLA Ops:
  12.0 46.0 %copy-start.1 = (bf16[640,1024]{1,0:T(8,128)(2,1)S(1)}, bf16[640,1024]{1,0:T(8,128)(2,1)}, u32[]{:S(2)}) copy-start(bf16[640,1024]{1,0:T(8,128)(2,1)} %constant.33.clone.table_hbm) | copy-start | bytes 3932164
  12.0 46.0 %copy-start.2 = (bf16[128,256]{1,0:T(8,128)(2,1)S(1)}, bf16[128,256]{1,0:T(8,128)(2,1)}, u32[]{:S(2)}) copy-start(bf16[128,256]{1,0:T(8,128)(2,1)} %constant.31.clone.inverse_hbm) | copy-start | bytes 196612
  12.0 46.0 %copy-start.3 = (bf16[512,256]{1,0:T(8,128)(2,1)S(1)}, bf16[512,256]{1,0:T(8,128)(2,1)}, u32[]{:S(2)}) copy-start(bf16[512,256]{1,0:T(8,128)(2,1)} %constant.30.clone.forward_hbm) | copy-start | bytes 786436
  12.0 46.0 %copy-start.4 = (f32[32,640]{1,0:T(8,128)S(1)}, f32[32,640]{1,0:T(8,128)}, u32[]{:S(2)}) copy-start(f32[32,640]{1,0:T(8,128)} %constant.32.clone.response_hbm) | copy-start | bytes 245764
  12.0 46.0 %copy-start.6 = (s32[16]{0:T(128)S(1)}, s32[16]{0:T(128)}, u32[]{:S(2)}) copy-start(s32[16]{0:T(128)} %slot_ref.1) | copy-start | bytes 196
  12.0 51.1 %all-to-all-start = ((bf16[16,168,128]{2,1,0:T(8,128)(2,1)}), bf16[16,168,128]{2,1,0:T(8,128)(2,1)S(1)}, u32[]{:S(2)}, u32[]{:S(2)}) async-start(bf16[16,168,128]{2,1,0:T(8,128)(2,1)} %second.1), calls=%async_computation | async-start | bytes 1376256 | tf_op jit(solution)/shard_map/all_to_all | solution.py:574
  18.7 7.7 %collective-permute-start = (bf16[2,216,128]{2,1,0:T(8,128)(2,1)S(1)}, bf16[2,216,128]{2,1,0:T(8,128)(2,1)S(1)}, u32[]{:S(2)}, u32[]{:S(2)}) collective-permute-start(bf16[2,216,128]{2,1,0:T(8,128)(2,1)S(1)} %get-tuple-element.29), channel_id=1, source_target_pairs={{0,2},{1,3},{2,0},{3,1},{4,6},{5,7},{6,4},{7,5},{8,10},{9,11},{10,... | collective-permute-start | bytes 331784 | tf_op jit(solution)/shard_map/ppermute | solution.py:557
  19.9 25.6 %collective-permute-start.1 = (bf16[2,216,128]{2,1,0:T(8,128)(2,1)S(1)}, bf16[2,216,128]{2,1,0:T(8,128)(2,1)S(1)}, u32[]{:S(2)}, u32[]{:S(2)}) collective-permute-start(bf16[2,216,128]{2,1,0:T(8,128)(2,1)S(1)} %get-tuple-element.30), channel_id=1, source_target_pairs={{0,4},{1,5},{2,6},{3,7},{4,8},{5,9},{6,10},{7,11},{8,12},{9,13},{1... | collective-permute-start | bytes 331784 | tf_op jit(solution)/shard_map/ppermute | solution.py:557
  21.1 26.8 %collective-permute-start.2 = (bf16[2,216,128]{2,1,0:T(8,128)(2,1)S(1)}, bf16[2,216,128]{2,1,0:T(8,128)(2,1)S(1)}, u32[]{:S(2)}, u32[]{:S(2)}) collective-permute-start(bf16[2,216,128]{2,1,0:T(8,128)(2,1)S(1)} %get-tuple-element.31), channel_id=1, source_target_pairs={{0,6},{1,7},{2,4},{3,5},{4,10},{5,11},{6,8},{7,9},{8,14},{9,15},{1... | collective-permute-start | bytes 331784 | tf_op jit(solution)/shard_map/ppermute | solution.py:557
  22.2 28.0 %collective-permute-start.3 = (bf16[2,216,128]{2,1,0:T(8,128)(2,1)S(1)}, bf16[2,216,128]{2,1,0:T(8,128)(2,1)S(1)}, u32[]{:S(2)}, u32[]{:S(2)}) collective-permute-start(bf16[2,216,128]{2,1,0:T(8,128)(2,1)S(1)} %get-tuple-element.32), channel_id=1, source_target_pairs={{0,8},{1,9},{2,10},{3,11},{4,12},{5,13},{6,14},{7,15},{8,0},{9,1},... | collective-permute-start | bytes 331784 | tf_op jit(solution)/shard_map/ppermute | solution.py:557
  23.4 29.2 %collective-permute-start.4 = (bf16[2,216,128]{2,1,0:T(8,128)(2,1)S(1)}, bf16[2,216,128]{2,1,0:T(8,128)(2,1)S(1)}, u32[]{:S(2)}, u32[]{:S(2)}) collective-permute-start(bf16[2,216,128]{2,1,0:T(8,128)(2,1)S(1)} %get-tuple-element.33), channel_id=1, source_target_pairs={{0,10},{1,11},{2,8},{3,9},{4,14},{5,15},{6,12},{7,13},{8,2},{9,3},... | collective-permute-start | bytes 331784 | tf_op jit(solution)/shard_map/ppermute | solution.py:557
  26.4 26.2 %collective-permute-start.5 = (bf16[2,216,128]{2,1,0:T(8,128)(2,1)S(1)}, bf16[2,216,128]{2,1,0:T(8,128)(2,1)S(1)}, u32[]{:S(2)}, u32[]{:S(2)}) collective-permute-start(bf16[2,216,128]{2,1,0:T(8,128)(2,1)S(1)} %get-tuple-element.34), channel_id=1, source_target_pairs={{0,12},{1,13},{2,14},{3,15},{4,0},{5,1},{6,2},{7,3},{8,4},{9,5},{1... | collective-permute-start | bytes 331784 | tf_op jit(solution)/shard_map/ppermute | solution.py:557
  45.5 9.9 %collective-permute-start.6 = (bf16[2,216,128]{2,1,0:T(8,128)(2,1)S(1)}, bf16[2,216,128]{2,1,0:T(8,128)(2,1)S(1)}, u32[]{:S(2)}, u32[]{:S(2)}) collective-permute-start(bf16[2,216,128]{2,1,0:T(8,128)(2,1)S(1)} %get-tuple-element.35), channel_id=1, source_target_pairs={{0,14},{1,15},{2,12},{3,13},{4,2},{5,3},{6,0},{7,1},{8,6},{9,7},{1... | collective-permute-start | bytes 331784 | tf_op jit(solution)/shard_map/ppermute | solution.py:557
  55.5 8.5 %copy-start.5 = (f32[32,512]{1,0:T(8,128)S(1)}, f32[32,512]{1,0:T(8,128)}, u32[]{:S(2)}) copy-start(f32[32,512]{1,0:T(8,128)} %constant.34.clone.response_hbm) | copy-start | bytes 196612
  55.5 2.5 %collective-permute-start.7 = (bf16[8,216,128]{2,1,0:T(8,128)(2,1)S(1)}, bf16[8,216,128]{2,1,0:T(8,128)(2,1)S(1)}, u32[]{:S(2)}, u32[]{:S(2)}) collective-permute-start(bf16[8,216,128]{2,1,0:T(8,128)(2,1)S(1)} %repack.1), channel_id=1, source_target_pairs={{0,1},{1,0},{2,3},{3,2},{4,5},{5,4},{6,7},{7,6},{8,9},{9,8},{10,11... | collective-permute-start | bytes 1327112 | tf_op jit(solution)/shard_map/ppermute | solution.py:585
  62.0 1.1 %copy-start = (bf16[672,1024]{1,0:T(8,128)(2,1)}, bf16[672,1024]{1,0:T(8,128)(2,1)S(1)}, u32[]{:S(2)}) copy-start(bf16[672,1024]{1,0:T(8,128)(2,1)S(1)} %get-tuple-element.38.odd_hbm) | copy-start | bytes 4128772
  63.1 0.9 %copy-start.7 = (bf16[16,168,128]{2,1,0:T(8,128)(2,1)}, bf16[16,168,128]{2,1,0:T(8,128)(2,1)S(1)}, u32[]{:S(2)}) copy-start(bf16[16,168,128]{2,1,0:T(8,128)(2,1)S(1)} %all-to-all-done.arrived_hbm) | copy-start | bytes 2064388
